TPU v7x, 1024 devices: a whole 4x4x32 slice. The times are simulated.
1024 devices in a mesh: dp: 128 (over z, x_hi, core), zero: 8 (over y, x_lo).
Axes of the slice: x: 4 (x_hi: 2, x_lo: 2; x = x_hi * 2 + x_lo), y: 4, z: 32, core: 2. Of those that a mesh axis runs over, the one named last changes fastest.
Arguments:
- pre_acts: bfloat16 [131072, 2560], P(('dp', 'zero')), may hold values from -6 to 6
- cotangent: bfloat16 [131072, 640], P(('dp', 'zero')), may hold values from -24 to 24
- w_out: bfloat16 [1280, 640], P('zero'), may hold values from -0.25 to 0.25
Outputs:
- d_pre: bfloat16 [131072, 2560], P(('dp', 'zero'))
- d_w: float32 [8, 102400], P('zero', 'dp')
All inputs are finite; a program needn't handle non-finite values.
Results may differ from a plain program's by a relative error of at most 0.0028.
Values may be sent and summed in bfloat16 or wider, within the bound.
No kernel may reach another device: no remote copies, remote signals or barrier semaphores. Data moves between devices by JAX's collectives and lax.ppermute only.
A program may use at most 32 MiB of HBM per device.

v0:
```python
import math

import jax
import jax.numpy as jnp
from jax import lax
from jax.sharding import PartitionSpec as P

D = 640
FFH = 1280


def body(pre_acts, cotangent, w_out):
    n_zero = lax.axis_size("zero")
    n_data = lax.axis_size("dp")
    tokens_all = pre_acts.shape[0] * n_data * n_zero
    scale = 1.0 / math.sqrt(tokens_all)
    value = pre_acts[:, :FFH].astype(jnp.float32)
    gate = pre_acts[:, FFH:].astype(jnp.float32)
    cdf = 0.5 * (1.0 + jax.scipy.special.erf(gate / math.sqrt(2.0)))
    act = gate * cdf
    hidden = (value * act).astype(jnp.bfloat16)
    d_hidden = jnp.einsum(
        "td,hd->th",
        cotangent,
        lax.all_gather(w_out, "zero", axis=0, tiled=True),
        preferred_element_type=jnp.float32,
    )
    dens = jnp.exp(-0.5 * gate * gate) / math.sqrt(2.0 * math.pi)
    d_value = d_hidden * act
    d_gate = d_hidden * value * (cdf + gate * dens)
    d_pre = jnp.concatenate([d_value, d_gate], axis=1).astype(jnp.bfloat16)
    own_rows = FFH // n_zero
    flat_len = own_rows * D
    piece_len = flat_len // n_data
    owned = lax.psum_scatter(
        jnp.einsum("th,td->hd", hidden, cotangent, preferred_element_type=jnp.float32) * scale,
        "zero",
        scatter_dimension=0,
        tiled=True,
    )
    blocks = owned.reshape(n_data, piece_len)
    d_w = lax.psum_scatter(blocks, "dp", scatter_dimension=0, tiled=True)
    return (d_pre, d_w)


def solution(mesh):
    return jax.shard_map(
        body,
        mesh=mesh,
        in_specs=(P(("dp", "zero"), None), P(("dp", "zero"), None), P("zero", None)),
        out_specs=(P(("dp", "zero"), None), P("zero", "dp")),
        check_vma=False,
    )
```

profile of v0, /device:TPU:8, one launch (start us, length us, event | category | flops | bytes accessed | tf_op | source)
XLA Modules:
  0.0 1151.1 jit_solution(8565058311465900738)
XLA Ops:
  7.2 0.0 copy-start
  7.2 0.0 reduce-scatter.2.cloned.1.call-start
  7.2 0.9 copy-done
  8.1 3.4 convolution_multiply_fusion
  11.5 0.0 copy-start.1
  11.5 0.0 reduce-scatter.2.cloned.1.call-update
  11.5 0.0 all-gather.2.cloned.1.call-start
  11.6 0.7 all-gather.2.cloned.1.call-update
  12.3 0.0 all-reduce.3.cloned.1.call-start
  12.3 1.3 dynamic-slice
  13.7 96.3 %reduce-scatter.2.cloned.1.call-done = f32[160,640]{1,0:T(8,128)} async-done(((f32[1280,640]{1,0:T(8,128)}), f32[160,640]{1,0:T(8,128)}) %reduce-scatter.2.cloned.1.call-update) | async-done | bytes 409616 | tf_op jit(solution)/shard_map/reduce_scatter | solution.py:35
  110.0 2.1 reshape.7
  112.1 0.0 all-reduce.3.cloned.1.call-update
  112.1 61.4 %all-gather.2.cloned.1.call-done = bf16[1280,640]{1,0:T(8,128)(2,1)} async-done(((bf16[160,640]{1,0:T(8,128)(2,1)}), bf16[1280,640]{1,0:T(8,128)(2,1)}) %all-gather.2.cloned.1.call-update) | async-done | bytes 1638416 | tf_op jit(solution)/shard_map/all_gather | solution.py:25
  173.5 0.0 copy-done.1
  173.5 2.1 multiply_convert_fusion
  175.6 0.9 pad_maximum_fusion
  176.5 966.1 %all-reduce.3.cloned.1.call-done = f32[128,800]{1,0:T(8,128)} async-done(((f32[128,800]{1,0:T(8,128)}), f32[128,800]{1,0:T(8,128)}) %all-reduce.3.cloned.1.call-update) | async-done | bytes 409616
  1142.6 2.0 constant_dynamic-slice_fusion
Async XLA Ops:
  7.2 0.9 copy-start
  7.2 102.8 %reduce-scatter.2.cloned.1.call-start = ((), (), s32[]{:S(2)}) async-start(), calls=%async_computation.2 | async-start | bytes 3686400 | tf_op jit(solution)/shard_map/reduce_scatter | solution.py:35
  11.5 162.1 %copy-start.1 = (bf16[128,2560]{1,0:T(8,128)(2,1)S(1)}, bf16[128,2560]{1,0:T(8,128)(2,1)}, u32[]{:S(2)}) copy-start(bf16[128,2560]{1,0:T(8,128)(2,1)} %param.3) | copy-start | bytes 1966084
  11.5 162.0 %all-gather.2.cloned.1.call-start = ((), (), s32[]{:S(2)}) async-start(), calls=%async_computation.1 | async-start | bytes 1843200 | tf_op jit(solution)/shard_map/all_gather | solution.py:25
  12.3 1130.3 %all-reduce.3.cloned.1.call-start = ((), (), s32[]{:S(2)}) async-start(), calls=%async_computation.3 | async-start | bytes 917504
Sparse Core Ops, SparseCore 0:
  11.6 98.2 reduce-scatter.1
  112.6 60.8 all-gather.1
  177.0 965.4 all-reduce.2
where the time goes:
time: 1150 us
  waiting for transfers between devices  1120 us (97%)
  between operations  13.8 us (1%)
    unnamed x4, waiting for transfers between devices  967 us
    reduce_scatter x1, waiting for transfers between devices, body(): lax.psum_scatter(jnp.einsum('th,td->hd', hidden, cotangent, preferred_ele...  96.3 us
    all_gather x1, waiting for transfers between devices, body(): lax.all_gather(w_out, 'zero', axis=0, tiled=True)  61.4 us
  transfers between devices with their start and end apart: 3, of which 3 were waited for; matrix products, arithmetic and copies ran while one was open for 1% of the time, Pallas kernels for 0%

commit v1 on v0

v1 whole, which is shorter than its diff:
```python
import math

import jax
import jax.numpy as jnp
from jax import lax
from jax.experimental import pallas as pl
from jax.experimental.pallas import tpu as pltpu
from jax.sharding import Mesh, PartitionSpec as P


D = 640
FFH = 1280
OWN = 160
GROUP = 8
TOK = 128
LANES = 128
COLS = D // LANES
FAR = 32
NEAR = 4
PIECE = 800
ROWS = 8
GROUP_AXES = ("y", "xl")
NEAR_AXES = ("xh", "c")
FAR_AXES = ("z",)
DP_AXES = FAR_AXES + NEAR_AXES
VMEM = pl.BlockSpec(memory_space=pltpu.VMEM)
SMEM = pl.BlockSpec(memory_space=pltpu.SMEM)


def cdf_of(gate):
    return 0.5 * (1.0 + lax.erf(gate * (1.0 / math.sqrt(2.0))))


def outgoing_kernel(pre_ref, cot_ref, out_ref, ht_ref):
    for c in range(COLS):
        block = cot_ref[:, pl.ds(c * LANES, LANES)]
        for s in range(GROUP):
            out_ref[s, pl.ds(c * TOK, TOK), :] = block
    for j in range(FFH // LANES):
        cols = pl.ds(j * LANES, LANES)
        value = pre_ref[:, cols].astype(jnp.float32)
        gate = pre_ref[:, pl.ds(FFH + j * LANES, LANES)].astype(jnp.float32)
        hidden = value * (gate * cdf_of(gate))
        ht_ref[cols, :] = hidden.T.astype(jnp.bfloat16)
    for s in range(GROUP):
        out_ref[s, pl.ds(D, OWN), :] = ht_ref[pl.ds(s * OWN, OWN), :]


def factors_kernel(pre_ref, act_ref, slope_ref):
    for j in range(FFH // LANES):
        cols = pl.ds(j * LANES, LANES)
        value = pre_ref[:, cols].astype(jnp.float32)
        gate = pre_ref[:, pl.ds(FFH + j * LANES, LANES)].astype(jnp.float32)
        cdf = cdf_of(gate)
        dens = jnp.exp(-0.5 * gate * gate) * (1.0 / math.sqrt(2.0 * math.pi))
        act_ref[:, cols] = gate * cdf
        slope_ref[:, cols] = value * (cdf + gate * dens)


def products_kernel(scale, near_ref, in_ref, w_ref, dh_ref, own_ref, *refs):
    outs, flat_ref, parts_ref = refs[: NEAR - 1], refs[-2], refs[-1]
    cots = jnp.concatenate(
        [
            jnp.concatenate([in_ref[s, pl.ds(c * TOK, TOK), :] for c in range(COLS)], axis=1)
            for s in range(GROUP)
        ],
        axis=0,
    )
    dht = lax.dot_general(w_ref[...], cots, (((1,), (1,)), ((), ())), preferred_element_type=jnp.float32)
    for s in range(GROUP):
        dh_ref[s] = dht[:, s * TOK : (s + 1) * TOK]
    ht = jnp.concatenate([in_ref[s, pl.ds(D, OWN), :] for s in range(GROUP)], axis=1)
    total = jnp.dot(ht, cots, preferred_element_type=jnp.float32) * scale
    for c in range(COLS):
        flat_ref[pl.ds(c, OWN, stride=COLS), :] = total[:, c * LANES : (c + 1) * LANES]
    flat_ref[pl.ds(OWN * COLS, ROWS), :] = jnp.zeros((ROWS, LANES), jnp.float32)
    for far in range(FAR):
        for near in range(NEAR):
            first = (far * NEAR + near) * PIECE // LANES
            parts_ref[near, far] = flat_ref[pl.ds(first, ROWS), :]
    mine = near_ref[0]
    own_ref[...] = parts_ref[mine]
    for j in range(1, NEAR):
        outs[j - 1][...] = parts_ref[jnp.bitwise_xor(mine, j)].astype(jnp.bfloat16)


def near_sum_kernel(own_ref, *refs):
    total = own_ref[...]
    for ref in refs[:-1]:
        total += ref[...].astype(jnp.float32)
    refs[-1][...] = total.astype(jnp.bfloat16)


def d_pre_kernel(dh_ref, act_ref, slope_ref, out_ref):
    for j in range(FFH // LANES):
        cols = pl.ds(j * LANES, LANES)
        dh = dh_ref[cols, :].T
        out_ref[:, cols] = (dh * act_ref[:, cols]).astype(jnp.bfloat16)
        out_ref[:, pl.ds(FFH + j * LANES, LANES)] = (dh * slope_ref[:, cols]).astype(jnp.bfloat16)


def far_sum_kernel(near_ref, got_ref, out_ref, line_ref):
    total = jnp.zeros((ROWS, LANES), jnp.float32)
    for far in range(FAR):
        total += got_ref[far].astype(jnp.float32)
    for row in range(ROWS):
        line_ref[:, pl.ds(row * LANES, LANES)] = total[row : row + 1, :]
    for near in range(NEAR):

        @pl.when(near_ref[0] == near)
        def _():
            out_ref[...] = line_ref[:, pl.ds(near * PIECE % LANES, PIECE)]


def call(kernel, out, *args, flops=0, scratch=()):
    outs = out if isinstance(out, tuple) else (out,)
    moved = sum(a.size * a.dtype.itemsize for a in args) + sum(o.size * o.dtype.itemsize for o in outs)
    return pl.pallas_call(
        kernel,
        out_shape=out,
        in_specs=[SMEM if a.dtype == jnp.int32 else VMEM for a in args],
        out_specs=(VMEM,) * len(outs) if isinstance(out, tuple) else VMEM,
        compiler_params=pltpu.CompilerParams(vmem_limit_bytes=16 << 20),
        cost_estimate=pl.CostEstimate(flops=flops, bytes_accessed=moved, transcendentals=0),
        scratch_shapes=list(scratch),
    )(*args)


def body(pre_acts, cotangent, w_out):
    scale = 1.0 / math.sqrt(TOK * GROUP * NEAR * FAR)
    bf16, f32 = jnp.bfloat16, jnp.float32
    S = jax.ShapeDtypeStruct
    near = (lax.axis_index("xh") * 2 + lax.axis_index("c")).astype(jnp.int32).reshape(1)

    outgoing = call(
        outgoing_kernel, S((GROUP, D + OWN, TOK), bf16), pre_acts, cotangent,
        scratch=[pltpu.VMEM((FFH, TOK), bf16)],
    )
    incoming = lax.all_to_all(outgoing, GROUP_AXES, 0, 0)
    block = (FAR, ROWS, LANES)
    dh, own, *parts = call(
        lambda *refs: products_kernel(scale, *refs),
        (S((GROUP, OWN, TOK), f32), S(block, f32)) + (S(block, bf16),) * (NEAR - 1),
        near, incoming, w_out,
        flops=4 * OWN * D * TOK * GROUP,
        scratch=[pltpu.VMEM((OWN * COLS + ROWS, LANES), f32), pltpu.VMEM((NEAR,) + block, f32)],
    )
    dh = lax.all_to_all(dh, GROUP_AXES, 0, 0)
    parts = [lax.ppermute(part, NEAR_AXES, [(i, i ^ (j + 1)) for i in range(NEAR)]) for j, part in enumerate(parts)]
    summed = call(near_sum_kernel, S(block, bf16), own, *parts)
    got = lax.all_to_all(summed, FAR_AXES, 0, 0)
    act, slope = call(factors_kernel, (S((TOK, FFH), f32),) * 2, pre_acts)
    d_pre = call(d_pre_kernel, S((TOK, 2 * FFH), bf16), dh.reshape(FFH, TOK), act, slope)
    d_w = call(
        far_sum_kernel, S((1, PIECE), f32), near, got, scratch=[pltpu.VMEM((1, ROWS * LANES), f32)]
    )
    return (d_pre, d_w)


def solution(mesh):
    fine = Mesh(mesh.devices.reshape(FAR, 2, 2, 4, 2), DP_AXES + GROUP_AXES)
    return jax.shard_map(
        body,
        mesh=fine,
        in_specs=(P(DP_AXES + GROUP_AXES, None), P(DP_AXES + GROUP_AXES, None), P(GROUP_AXES, None)),
        out_specs=(P(DP_AXES + GROUP_AXES, None), P(GROUP_AXES, DP_AXES)),
        check_vma=False,
    )
```

time: 1150 us -> 108 us (0.09)
  waiting for transfers between devices: 1120 us -> 42.4 us
  starting transfers between devices: 0.12 us -> 56.6 us
  between operations: 13.8 us -> 0.7 us
    unnamed x4 -> x0, waiting for transfers between devices: 967 us -> none
    reduce_scatter x1 -> x0, waiting for transfers between devices: 96.3 us -> none  [body(): lax.psum_scatter(jnp.einsum('th,td->hd', hidden, cotangent, preferred_ele...]
    all_gather x1 -> x0, waiting for transfers between devices: 61.4 us -> none  [body(): lax.all_gather(w_out, 'zero', axis=0, tiled=True)]
    all_to_all x0 -> x3, starting transfers between devices: none -> 47.5 us  [the longest x1 25.4 us: body(): got = lax.all_to_all(summed, FAR_AXES, 0, 0)]
    all_to_all x0 -> x3, waiting for transfers between devices: none -> 40.3 us  [the longest x1 24.8 us: body(): got = lax.all_to_all(summed, FAR_AXES, 0, 0)]
  transfers between devices with their start and end apart: 3 -> 6, of which waited for: 3 -> 4; matrix products, arithmetic and copies ran while one was open for 1% -> 0% of each run, Pallas kernels for 0% -> 2%
where the time goes in v1:
time: 108 us; the launch traced here: 107 us
  starting transfers between devices  56.6 us (52%)
  waiting for transfers between devices  42.4 us (39%)
  Pallas kernels  5.82 us (5%)
  local copies, waits for them, and re-layouts  2.01 us (2%)
    all_to_all x1, starting transfers between devices, body(): got = lax.all_to_all(summed, FAR_AXES, 0, 0)  25.4 us
    all_to_all x1, waiting for transfers between devices, body(): got = lax.all_to_all(summed, FAR_AXES, 0, 0)  24.8 us
    all_to_all x1, starting transfers between devices, body(): incoming = lax.all_to_all(outgoing, GROUP_AXES, 0, 0)  16.7 us
    all_to_all x1, waiting for transfers between devices, body(): incoming = lax.all_to_all(outgoing, GROUP_AXES, 0, 0)  15.5 us
    ppermute x3, starting transfers between devices, body(): lax.ppermute(part, NEAR_AXES, [(i, i ^ j + 1) for i in range(NEAR)])  9.08 us
    pallas_call x6, Pallas kernels, call(): pl.pallas_call(kernel, out_shape=out, in_specs=[SMEM if a.dtype == jnp.in...  5.82 us
    all_to_all x1, starting transfers between devices, body(): dh = lax.all_to_all(dh, GROUP_AXES, 0, 0)  5.42 us
  transfers between devices with their start and end apart: 6, of which 4 were waited for; matrix products, arithmetic and copies ran while one was open for 0% of the time, Pallas kernels for 2%

profile of v1, /device:TPU:8, one launch (start us, length us, event | category | flops | bytes accessed | tf_op | source)
XLA Modules:
  0.0 107.5 jit_solution(17040401948351799924)
XLA Ops:
  0.6 0.0 copy-start
  0.6 1.1 %copy-done = bf16[128,2560]{1,0:T(8,128)(2,1)S(1)} copy-done((bf16[128,2560]{1,0:T(8,128)(2,1)S(1)}, bf16[128,2560]{1,0:T(8,128)(2,1)}, u32[]{:S(2)}) %copy-start) | copy-done | bytes 655384
  1.7 0.0 copy-start.3
  1.7 0.9 copy-done.3
  2.6 1.6 %shard_map.50 = bf16[8,800,128]{2,1,0:T(8,128)(2,1)} custom-call(bf16[128,2560]{1,0:T(8,128)(2,1)S(1)} %copy-done, bf16[128,640]{1,0:T(8,128)(2,1)S(1)} %copy-done.3), custom_call_target="tpu_custom_call" | custom-call | bytes 2457600 | tf_op jit(solution)/shard_map/pallas_call | solution.py:118
  4.3 0.0 copy-start.2
  4.3 16.7 %all-to-all-start = ((bf16[8,800,128]{2,1,0:T(8,128)(2,1)}), bf16[8,800,128]{2,1,0:T(8,128)(2,1)S(1)}, u32[]{:S(2)}, u32[]{:S(2)}) async-start(bf16[8,800,128]{2,1,0:T(8,128)(2,1)} %shard_map.50), calls=%async_computation | async-start | bytes 3276800 | tf_op jit(solution)/shard_map/all_to_all | solution.py:139
  21.0 15.5 %all-to-all-done.refs_1_ = bf16[8,800,128]{2,1,0:T(8,128)(2,1)S(1)} async-done(((bf16[8,800,128]{2,1,0:T(8,128)(2,1)}), bf16[8,800,128]{2,1,0:T(8,128)(2,1)S(1)}, u32[]{:S(2)}, u32[]{:S(2)}) %all-to-all-start) | async-done | bytes 1638432 | tf_op jit(solution)/shard_map/all_to_all | solution.py:139
  36.5 0.0 copy-done.2
  36.5 0.0 copy-start.1
  36.5 1.5 %shard_map.51 = (f32[8,160,128]{2,1,0:T(8,128)}, f32[32,8,128]{2,1,0:T(8,128)S(1)}, bf16[32,8,128]{2,1,0:T(8,128)(2,1)S(1)}, bf16[32,8,128]{2,1,0:T(8,128)(2,1)S(1)}, bf16[32,8,128]{2,1,0:T(8,128)(2,1)S(1)}) custom-call(s32[1]{0:T(128)} %bitcast.refs_0_.near_ref, bf16[8,800,128]{2,1,0:T(8,128)(2,1)S(1)} %all-to-all-done.refs_1_, bf16[160,640]{1,0:T(8,128)(2,1)S(1)} %copy-done.2), custom_call_target="tpu_custom_call" | custom-call | flops 419430400 | bytes 2826244 | tf_op jit(solution)/shard_map/pallas_call | solution.py:118
  38.0 5.4 %all-to-all-start.1 = ((f32[8,160,128]{2,1,0:T(8,128)}), f32[8,160,128]{2,1,0:T(8,128)S(1)}, u32[]{:S(2)}, u32[]{:S(2)}) async-start(f32[8,160,128]{2,1,0:T(8,128)} %get-tuple-element.9), calls=%async_computation.1 | async-start | bytes 1310720 | tf_op jit(solution)/shard_map/all_to_all | solution.py:148
  43.4 1.9 %collective-permute-start = (bf16[32,8,128]{2,1,0:T(8,128)(2,1)S(1)}, bf16[32,8,128]{2,1,0:T(8,128)(2,1)S(1)}, u32[]{:S(2)}, u32[]{:S(2)}) collective-permute-start(bf16[32,8,128]{2,1,0:T(8,128)(2,1)S(1)} %get-tuple-element.13), channel_id=1, source_target_pairs={{0,8},{8,0},{16,24},{24,16},{1,9},{9,1},{17,25},{25,17},{2,10},{10... | collective-permute-start | bytes 196616 | tf_op jit(solution)/shard_map/ppermute | solution.py:149
  45.3 1.9 %collective-permute-start.1 = (bf16[32,8,128]{2,1,0:T(8,128)(2,1)S(1)}, bf16[32,8,128]{2,1,0:T(8,128)(2,1)S(1)}, u32[]{:S(2)}, u32[]{:S(2)}) collective-permute-start(bf16[32,8,128]{2,1,0:T(8,128)(2,1)S(1)} %get-tuple-element.14), channel_id=1, source_target_pairs={{0,16},{8,24},{16,0},{24,8},{1,17},{9,25},{17,1},{25,9},{2,18},{10... | collective-permute-start | bytes 196616 | tf_op jit(solution)/shard_map/ppermute | solution.py:149
  47.3 5.2 %collective-permute-start.2 = (bf16[32,8,128]{2,1,0:T(8,128)(2,1)S(1)}, bf16[32,8,128]{2,1,0:T(8,128)(2,1)S(1)}, u32[]{:S(2)}, u32[]{:S(2)}) collective-permute-start(bf16[32,8,128]{2,1,0:T(8,128)(2,1)S(1)} %get-tuple-element.15), channel_id=1, source_target_pairs={{0,24},{8,16},{16,8},{24,0},{1,25},{9,17},{17,9},{25,1},{2,26},{10... | collective-permute-start | bytes 196616 | tf_op jit(solution)/shard_map/ppermute | solution.py:149
  52.5 0.0 collective-permute-done.refs_0_
  52.5 0.7 collective-permute-done.1.refs_1_
  53.2 1.4 %collective-permute-done.2.refs_2_ = bf16[32,8,128]{2,1,0:T(8,128)(2,1)S(1)} collective-permute-done((bf16[32,8,128]{2,1,0:T(8,128)(2,1)S(1)}, bf16[32,8,128]{2,1,0:T(8,128)(2,1)S(1)}, u32[]{:S(2)}, u32[]{:S(2)}) %collective-permute-start.2) | collective-permute-done | bytes 65568 | tf_op jit(solution)/shard_map/ppermute | solution.py:149
  54.6 0.7 shard_map.54
  55.2 0.0 all-to-all-done.1
  55.2 25.4 %all-to-all-start.2 = ((bf16[32,8,128]{2,1,0:T(8,128)(2,1)}), bf16[32,8,128]{2,1,0:T(8,128)(2,1)S(1)}, u32[]{:S(2)}, u32[]{:S(2)}) async-start(bf16[32,8,128]{2,1,0:T(8,128)(2,1)} %shard_map.54), calls=%async_computation.2 | async-start | bytes 131072 | tf_op jit(solution)/shard_map/all_to_all | solution.py:151
  80.6 0.0 copy-done.1
  80.6 0.3 shard_map.52
  81.0 1.1 %shard_map.53 = bf16[128,2560]{1,0:T(8,128)(2,1)} custom-call(f32[1280,128]{1,0:T(8,128)S(1)} %bitcast.2, f32[128,1280]{1,0:T(8,128)S(1)} %get-tuple-element.10.act_ref, f32[128,1280]{1,0:T(8,128)S(1)} %get-tuple-element.11.slope_ref), custom_call_target="tpu_custom_call" | custom-call | bytes 2621440 | tf_op jit(solution)/shard_map/pallas_call | solution.py:118
  82.0 24.8 %all-to-all-done.2.got_ref = bf16[32,8,128]{2,1,0:T(8,128)(2,1)S(1)} async-done(((bf16[32,8,128]{2,1,0:T(8,128)(2,1)}), bf16[32,8,128]{2,1,0:T(8,128)(2,1)S(1)}, u32[]{:S(2)}, u32[]{:S(2)}) %all-to-all-start.2) | async-done | bytes 65568 | tf_op jit(solution)/shard_map/all_to_all | solution.py:151
  106.8 0.6 shard_map.55
Async XLA Ops:
  0.6 1.1 %copy-start = (bf16[128,2560]{1,0:T(8,128)(2,1)S(1)}, bf16[128,2560]{1,0:T(8,128)(2,1)}, u32[]{:S(2)}) copy-start(bf16[128,2560]{1,0:T(8,128)(2,1)} %pre_ref.3) | copy-start | bytes 1966084
  1.7 0.9 copy-start.3
  4.3 32.2 %copy-start.2 = (bf16[160,640]{1,0:T(8,128)(2,1)S(1)}, bf16[160,640]{1,0:T(8,128)(2,1)}, u32[]{:S(2)}) copy-start(bf16[160,640]{1,0:T(8,128)(2,1)} %refs_2_.1) | copy-start | bytes 614404
  4.3 32.2 %all-to-all-start = ((bf16[8,800,128]{2,1,0:T(8,128)(2,1)}), bf16[8,800,128]{2,1,0:T(8,128)(2,1)S(1)}, u32[]{:S(2)}, u32[]{:S(2)}) async-start(bf16[8,800,128]{2,1,0:T(8,128)(2,1)} %shard_map.50), calls=%async_computation | async-start | bytes 3276800 | tf_op jit(solution)/shard_map/all_to_all | solution.py:139
  36.5 44.1 %copy-start.1 = (bf16[128,2560]{1,0:T(8,128)(2,1)S(1)}, bf16[128,2560]{1,0:T(8,128)(2,1)}, u32[]{:S(2)}) copy-start(bf16[128,2560]{1,0:T(8,128)(2,1)} %pre_ref.3) | copy-start | bytes 1966084
  38.0 17.2 %all-to-all-start.1 = ((f32[8,160,128]{2,1,0:T(8,128)}), f32[8,160,128]{2,1,0:T(8,128)S(1)}, u32[]{:S(2)}, u32[]{:S(2)}) async-start(f32[8,160,128]{2,1,0:T(8,128)} %get-tuple-element.9), calls=%async_computation.1 | async-start | bytes 1310720 | tf_op jit(solution)/shard_map/all_to_all | solution.py:148
  43.4 9.1 %collective-permute-start = (bf16[32,8,128]{2,1,0:T(8,128)(2,1)S(1)}, bf16[32,8,128]{2,1,0:T(8,128)(2,1)S(1)}, u32[]{:S(2)}, u32[]{:S(2)}) collective-permute-start(bf16[32,8,128]{2,1,0:T(8,128)(2,1)S(1)} %get-tuple-element.13), channel_id=1, source_target_pairs={{0,8},{8,0},{16,24},{24,16},{1,9},{9,1},{17,25},{25,17},{2,10},{10... | collective-permute-start | bytes 196616 | tf_op jit(solution)/shard_map/ppermute | solution.py:149
  45.3 7.9 %collective-permute-start.1 = (bf16[32,8,128]{2,1,0:T(8,128)(2,1)S(1)}, bf16[32,8,128]{2,1,0:T(8,128)(2,1)S(1)}, u32[]{:S(2)}, u32[]{:S(2)}) collective-permute-start(bf16[32,8,128]{2,1,0:T(8,128)(2,1)S(1)} %get-tuple-element.14), channel_id=1, source_target_pairs={{0,16},{8,24},{16,0},{24,8},{1,17},{9,25},{17,1},{25,9},{2,18},{10... | collective-permute-start | bytes 196616 | tf_op jit(solution)/shard_map/ppermute | solution.py:149
  47.3 7.3 %collective-permute-start.2 = (bf16[32,8,128]{2,1,0:T(8,128)(2,1)S(1)}, bf16[32,8,128]{2,1,0:T(8,128)(2,1)S(1)}, u32[]{:S(2)}, u32[]{:S(2)}) collective-permute-start(bf16[32,8,128]{2,1,0:T(8,128)(2,1)S(1)} %get-tuple-element.15), channel_id=1, source_target_pairs={{0,24},{8,16},{16,8},{24,0},{1,25},{9,17},{17,9},{25,1},{2,26},{10... | collective-permute-start | bytes 196616 | tf_op jit(solution)/shard_map/ppermute | solution.py:149
  55.2 51.6 %all-to-all-start.2 = ((bf16[32,8,128]{2,1,0:T(8,128)(2,1)}), bf16[32,8,128]{2,1,0:T(8,128)(2,1)S(1)}, u32[]{:S(2)}, u32[]{:S(2)}) async-start(bf16[32,8,128]{2,1,0:T(8,128)(2,1)} %shard_map.54), calls=%async_computation.2 | async-start | bytes 131072 | tf_op jit(solution)/shard_map/all_to_all | solution.py:151

commit v2 on v1

--- a/solution.py
+++ b/solution.py
@@ -22,6 +22,7 @@
 GROUP_AXES = ("y", "xl")
 NEAR_AXES = ("xh", "c")
 FAR_AXES = ("z",)
+FAR_ORDER = [(i + 16) % FAR for i in range(FAR)]
 DP_AXES = FAR_AXES + NEAR_AXES
 VMEM = pl.BlockSpec(memory_space=pltpu.VMEM)
 SMEM = pl.BlockSpec(memory_space=pltpu.SMEM)
@@ -31,7 +32,7 @@
     return 0.5 * (1.0 + lax.erf(gate * (1.0 / math.sqrt(2.0))))
 
 
-def outgoing_kernel(pre_ref, cot_ref, out_ref, ht_ref):
+def outgoing_kernel(_, pre_ref, cot_ref, out_ref, ht_ref):
     for c in range(COLS):
         block = cot_ref[:, pl.ds(c * LANES, LANES)]
         for s in range(GROUP):
@@ -77,21 +78,22 @@
     for far in range(FAR):
         for near in range(NEAR):
             first = (far * NEAR + near) * PIECE // LANES
-            parts_ref[near, far] = flat_ref[pl.ds(first, ROWS), :]
+            parts_ref[near, FAR_ORDER.index(far)] = flat_ref[pl.ds(first, ROWS), :]
     mine = near_ref[0]
     own_ref[...] = parts_ref[mine]
     for j in range(1, NEAR):
         outs[j - 1][...] = parts_ref[jnp.bitwise_xor(mine, j)].astype(jnp.bfloat16)
 
 
-def near_sum_kernel(own_ref, *refs):
+def near_sum_kernel(_, own_ref, *refs):
     total = own_ref[...]
     for ref in refs[:-1]:
         total += ref[...].astype(jnp.float32)
     refs[-1][...] = total.astype(jnp.bfloat16)
 
 
-def d_pre_kernel(dh_ref, act_ref, slope_ref, out_ref):
+def d_pre_kernel(dh_ref, act_ref, slope_ref, out_ref, done_ref):
+    done_ref[...] = jnp.zeros_like(done_ref)
     for j in range(FFH // LANES):
         cols = pl.ds(j * LANES, LANES)
         dh = dh_ref[cols, :].T
@@ -133,7 +135,7 @@
     near = (lax.axis_index("xh") * 2 + lax.axis_index("c")).astype(jnp.int32).reshape(1)
 
     outgoing = call(
-        outgoing_kernel, S((GROUP, D + OWN, TOK), bf16), pre_acts, cotangent,
+        outgoing_kernel, S((GROUP, D + OWN, TOK), bf16), near, pre_acts, cotangent,
         scratch=[pltpu.VMEM((FFH, TOK), bf16)],
     )
     incoming = lax.all_to_all(outgoing, GROUP_AXES, 0, 0)
@@ -147,10 +149,10 @@
     )
     dh = lax.all_to_all(dh, GROUP_AXES, 0, 0)
     parts = [lax.ppermute(part, NEAR_AXES, [(i, i ^ (j + 1)) for i in range(NEAR)]) for j, part in enumerate(parts)]
-    summed = call(near_sum_kernel, S(block, bf16), own, *parts)
-    got = lax.all_to_all(summed, FAR_AXES, 0, 0)
     act, slope = call(factors_kernel, (S((TOK, FFH), f32),) * 2, pre_acts)
-    d_pre = call(d_pre_kernel, S((TOK, 2 * FFH), bf16), dh.reshape(FFH, TOK), act, slope)
+    d_pre, done = call(d_pre_kernel, (S((TOK, 2 * FFH), bf16), S((ROWS, LANES), f32)), dh.reshape(FFH, TOK), act, slope)
+    summed = call(near_sum_kernel, S(block, bf16), done, own, *parts)
+    got = lax.all_to_all(summed, "z", 0, 0, axis_index_groups=[FAR_ORDER])
     d_w = call(
         far_sum_kernel, S((1, PIECE), f32), near, got, scratch=[pltpu.VMEM((1, ROWS * LANES), f32)]
     )

time: 108 us -> 93.7 us (0.87)
  the two profiles are of different devices: /device:TPU:8 before, /device:TPU:1 now
where the time goes in v2:
time: 93.7 us; the launch traced here: 93.3 us
  blocking collectives  60 us (64%)
  starting transfers between devices  25.7 us (27%)
  Pallas kernels  4.07 us (4%)
  local copies, waits for them, and re-layouts  2.01 us (2%)
    all_to_all x1, blocking collectives, body(): got = lax.all_to_all(summed, 'z', 0, 0, axis_index_groups=[FAR_ORDER])  40.5 us
    ppermute x3, starting transfers between devices, body(): lax.ppermute(part, NEAR_AXES, [(i, i ^ j + 1) for i in range(NEAR)])  22.2 us
    all_to_all x1, blocking collectives, body(): incoming = lax.all_to_all(outgoing, GROUP_AXES, 0, 0)  19.5 us
    pallas_call x6, Pallas kernels, call(): pl.pallas_call(kernel, out_shape=out, in_specs=[SMEM if a.dtype == jnp.in...  4.07 us
    all_to_all x1, starting transfers between devices, body(): dh = lax.all_to_all(dh, GROUP_AXES, 0, 0)  3.54 us
    unnamed x8, local copies, waits for them, and re-layouts  2.01 us
  transfers between devices with their start and end apart: 4, of which 1 were waited for; matrix products, arithmetic and copies ran while one was open for 0% of the time, Pallas kernels for 2%

profile of v2, /device:TPU:1, one launch (start us, length us, event | category | flops | bytes accessed | tf_op | source)
XLA Modules:
  0.0 93.3 jit_solution(7073137395858683113)
XLA Ops:
  0.6 0.0 copy-start
  0.6 1.1 %copy-done = bf16[128,2560]{1,0:T(8,128)(2,1)S(1)} copy-done((bf16[128,2560]{1,0:T(8,128)(2,1)S(1)}, bf16[128,2560]{1,0:T(8,128)(2,1)}, u32[]{:S(2)}) %copy-start) | copy-done | bytes 655384
  1.7 0.0 copy-start.3
  1.7 0.9 copy-done.3
  2.6 0.4 shard_map.50
  3.1 0.0 copy-start.2
  3.1 19.5 %all_to_all.15.refs_1_ = bf16[8,800,128]{2,1,0:T(8,128)(2,1)S(1)} all-to-all(bf16[8,800,128]{2,1,0:T(8,128)(2,1)S(1)} %shard_map.50), channel_id=1, replica_groups=mesh['z'=32,'xh'=2,'c'=2,'y'=4,'xl'=2] {'y','xl'}, dimensions={0} | all-to-all | bytes 3276800 | tf_op jit(solution)/shard_map/all_to_all | solution.py:141
  22.6 0.0 copy-done.2
  22.6 0.0 copy-start.1
  22.6 1.5 %shard_map.51 = (f32[8,160,128]{2,1,0:T(8,128)}, f32[32,8,128]{2,1,0:T(8,128)S(1)}, bf16[32,8,128]{2,1,0:T(8,128)(2,1)S(1)}, bf16[32,8,128]{2,1,0:T(8,128)(2,1)S(1)}, bf16[32,8,128]{2,1,0:T(8,128)(2,1)S(1)}) custom-call(s32[1]{0:T(128)} %bitcast._.refs_0_.near_ref, bf16[8,800,128]{2,1,0:T(8,128)(2,1)S(1)} %all_to_all.15.refs_1_, bf16[160,640]{1,0:T(8,128)(2,1)S(1)} %copy-done.2), custom_call_target="tpu_custom_call" | custom-call | flops 419430400 | bytes 2826244 | tf_op jit(solution)/shard_map/pallas_call | solution.py:120
  24.1 3.5 %all-to-all-start.1 = ((f32[8,160,128]{2,1,0:T(8,128)}), f32[8,160,128]{2,1,0:T(8,128)S(1)}, u32[]{:S(2)}, u32[]{:S(2)}) async-start(f32[8,160,128]{2,1,0:T(8,128)} %get-tuple-element.11), calls=%async_computation.1 | async-start | bytes 1310720 | tf_op jit(solution)/shard_map/all_to_all | solution.py:150
  27.6 15.2 %collective-permute-start = (bf16[32,8,128]{2,1,0:T(8,128)(2,1)S(1)}, bf16[32,8,128]{2,1,0:T(8,128)(2,1)S(1)}, u32[]{:S(2)}, u32[]{:S(2)}) collective-permute-start(bf16[32,8,128]{2,1,0:T(8,128)(2,1)S(1)} %get-tuple-element.17), channel_id=1, source_target_pairs={{0,8},{8,0},{16,24},{24,16},{1,9},{9,1},{17,25},{25,17},{2,10},{10... | collective-permute-start | bytes 196616 | tf_op jit(solution)/shard_map/ppermute | solution.py:151
  42.9 1.9 %collective-permute-start.1 = (bf16[32,8,128]{2,1,0:T(8,128)(2,1)S(1)}, bf16[32,8,128]{2,1,0:T(8,128)(2,1)S(1)}, u32[]{:S(2)}, u32[]{:S(2)}) collective-permute-start(bf16[32,8,128]{2,1,0:T(8,128)(2,1)S(1)} %get-tuple-element.18), channel_id=1, source_target_pairs={{0,16},{8,24},{16,0},{24,8},{1,17},{9,25},{17,1},{25,9},{2,18},{10... | collective-permute-start | bytes 196616 | tf_op jit(solution)/shard_map/ppermute | solution.py:151
  44.8 5.0 %collective-permute-start.2 = (bf16[32,8,128]{2,1,0:T(8,128)(2,1)S(1)}, bf16[32,8,128]{2,1,0:T(8,128)(2,1)S(1)}, u32[]{:S(2)}, u32[]{:S(2)}) collective-permute-start(bf16[32,8,128]{2,1,0:T(8,128)(2,1)S(1)} %get-tuple-element.19), channel_id=1, source_target_pairs={{0,24},{8,16},{16,8},{24,0},{1,25},{9,17},{17,9},{25,1},{2,26},{10... | collective-permute-start | bytes 196616 | tf_op jit(solution)/shard_map/ppermute | solution.py:151
  49.9 0.0 copy-done.1
  49.9 0.3 shard_map.52
  50.2 0.0 all-to-all-done.1
  50.2 1.1 %shard_map.53 = (bf16[128,2560]{1,0:T(8,128)(2,1)}, f32[8,128]{1,0:T(8,128)S(1)}) custom-call(f32[1280,128]{1,0:T(8,128)S(1)} %bitcast.2, f32[128,1280]{1,0:T(8,128)S(1)} %get-tuple-element.12.act_ref, f32[128,1280]{1,0:T(8,128)S(1)} %get-tuple-element.13.slope_ref), custom_call_target="tpu_custom_call" | custom-call | bytes 2625536 | tf_op jit(solution)/shard_map/pallas_call | solution.py:120
  51.3 0.0 collective-permute-done.refs_0_
  51.3 0.0 collective-permute-done.1.refs_1_
  51.3 0.7 collective-permute-done.2.refs_2_
  52.1 40.5 %all_to_all.16.got_ref = bf16[32,8,128]{2,1,0:T(8,128)(2,1)S(1)} all-to-all(bf16[32,8,128]{2,1,0:T(8,128)(2,1)S(1)} %shard_map.54), channel_id=1, replica_groups={{512,544,576,608,640,672,704,736,768,800,832,864,896,928,960,992,0,32,6..., dimensions={0} | all-to-all | bytes 131072 | tf_op jit(solution)/shard_map/all_to_all | solution.py:155
  92.6 0.7 shard_map.55
  (1 shorter events, 0.0 us)
Async XLA Ops:
  0.6 1.1 %copy-start = (bf16[128,2560]{1,0:T(8,128)(2,1)S(1)}, bf16[128,2560]{1,0:T(8,128)(2,1)}, u32[]{:S(2)}) copy-start(bf16[128,2560]{1,0:T(8,128)(2,1)} %pre_ref.3) | copy-start | bytes 1966084
  1.7 0.9 copy-start.3
  3.1 19.5 %copy-start.2 = (bf16[160,640]{1,0:T(8,128)(2,1)S(1)}, bf16[160,640]{1,0:T(8,128)(2,1)}, u32[]{:S(2)}) copy-start(bf16[160,640]{1,0:T(8,128)(2,1)} %refs_2_.1) | copy-start | bytes 614404
  22.6 27.3 %copy-start.1 = (bf16[128,2560]{1,0:T(8,128)(2,1)S(1)}, bf16[128,2560]{1,0:T(8,128)(2,1)}, u32[]{:S(2)}) copy-start(bf16[128,2560]{1,0:T(8,128)(2,1)} %pre_ref.3) | copy-start | bytes 1966084
  24.1 26.1 %all-to-all-start.1 = ((f32[8,160,128]{2,1,0:T(8,128)}), f32[8,160,128]{2,1,0:T(8,128)S(1)}, u32[]{:S(2)}, u32[]{:S(2)}) async-start(f32[8,160,128]{2,1,0:T(8,128)} %get-tuple-element.11), calls=%async_computation.1 | async-start | bytes 1310720 | tf_op jit(solution)/shard_map/all_to_all | solution.py:150
  27.6 23.6 %collective-permute-start = (bf16[32,8,128]{2,1,0:T(8,128)(2,1)S(1)}, bf16[32,8,128]{2,1,0:T(8,128)(2,1)S(1)}, u32[]{:S(2)}, u32[]{:S(2)}) collective-permute-start(bf16[32,8,128]{2,1,0:T(8,128)(2,1)S(1)} %get-tuple-element.17), channel_id=1, source_target_pairs={{0,8},{8,0},{16,24},{24,16},{1,9},{9,1},{17,25},{25,17},{2,10},{10... | collective-permute-start | bytes 196616 | tf_op jit(solution)/shard_map/ppermute | solution.py:151
  42.9 8.4 %collective-permute-start.1 = (bf16[32,8,128]{2,1,0:T(8,128)(2,1)S(1)}, bf16[32,8,128]{2,1,0:T(8,128)(2,1)S(1)}, u32[]{:S(2)}, u32[]{:S(2)}) collective-permute-start(bf16[32,8,128]{2,1,0:T(8,128)(2,1)S(1)} %get-tuple-element.18), channel_id=1, source_target_pairs={{0,16},{8,24},{16,0},{24,8},{1,17},{9,25},{17,1},{25,9},{2,18},{10... | collective-permute-start | bytes 196616 | tf_op jit(solution)/shard_map/ppermute | solution.py:151
  44.8 7.2 %collective-permute-start.2 = (bf16[32,8,128]{2,1,0:T(8,128)(2,1)S(1)}, bf16[32,8,128]{2,1,0:T(8,128)(2,1)S(1)}, u32[]{:S(2)}, u32[]{:S(2)}) collective-permute-start(bf16[32,8,128]{2,1,0:T(8,128)(2,1)S(1)} %get-tuple-element.19), channel_id=1, source_target_pairs={{0,24},{8,16},{16,8},{24,0},{1,25},{9,17},{17,9},{25,1},{2,26},{10... | collective-permute-start | bytes 196616 | tf_op jit(solution)/shard_map/ppermute | solution.py:151

commit v3 on v2

--- a/solution.py
+++ b/solution.py
@@ -58,8 +58,7 @@
         slope_ref[:, cols] = value * (cdf + gate * dens)
 
 
-def products_kernel(scale, near_ref, in_ref, w_ref, dh_ref, own_ref, *refs):
-    outs, flat_ref, parts_ref = refs[: NEAR - 1], refs[-2], refs[-1]
+def products_kernel(scale, at_ref, in_ref, w_ref, dh_ref, keep_ref, give_ref, flat_ref, parts_ref):
     cots = jnp.concatenate(
         [
             jnp.concatenate([in_ref[s, pl.ds(c * TOK, TOK), :] for c in range(COLS)], axis=1)
@@ -79,17 +78,20 @@
         for near in range(NEAR):
             first = (far * NEAR + near) * PIECE // LANES
             parts_ref[near, FAR_ORDER.index(far)] = flat_ref[pl.ds(first, ROWS), :]
-    mine = near_ref[0]
-    own_ref[...] = parts_ref[mine]
-    for j in range(1, NEAR):
-        outs[j - 1][...] = parts_ref[jnp.bitwise_xor(mine, j)].astype(jnp.bfloat16)
+    core = lax.rem(at_ref[0], 2)
+    for half in range(2):
+        keep_ref[half] = parts_ref[half * 2 + core]
+        give_ref[half] = parts_ref[half * 2 + 1 - core]
 
 
-def near_sum_kernel(_, own_ref, *refs):
-    total = own_ref[...]
-    for ref in refs[:-1]:
-        total += ref[...].astype(jnp.float32)
-    refs[-1][...] = total.astype(jnp.bfloat16)
+def core_sum_kernel(at_ref, own_ref, got_ref, keep_ref, give_ref):
+    half = lax.div(at_ref[0], 2)
+    keep_ref[...] = own_ref[half] + got_ref[half]
+    give_ref[...] = (own_ref[1 - half] + got_ref[1 - half]).astype(jnp.bfloat16)
+
+
+def near_sum_kernel(_, own_ref, got_ref, out_ref):
+    out_ref[...] = (own_ref[...] + got_ref[...].astype(jnp.float32)).astype(jnp.bfloat16)
 
 
 def d_pre_kernel(dh_ref, act_ref, slope_ref, out_ref, done_ref):
@@ -101,7 +103,7 @@
         out_ref[:, pl.ds(FFH + j * LANES, LANES)] = (dh * slope_ref[:, cols]).astype(jnp.bfloat16)
 
 
-def far_sum_kernel(near_ref, got_ref, out_ref, line_ref):
+def far_sum_kernel(at_ref, got_ref, out_ref, line_ref):
     total = jnp.zeros((ROWS, LANES), jnp.float32)
     for far in range(FAR):
         total += got_ref[far].astype(jnp.float32)
@@ -109,7 +111,7 @@
         line_ref[:, pl.ds(row * LANES, LANES)] = total[row : row + 1, :]
     for near in range(NEAR):
 
-        @pl.when(near_ref[0] == near)
+        @pl.when(at_ref[0] == near)
         def _():
             out_ref[...] = line_ref[:, pl.ds(near * PIECE % LANES, PIECE)]
 
@@ -132,29 +134,31 @@
     scale = 1.0 / math.sqrt(TOK * GROUP * NEAR * FAR)
     bf16, f32 = jnp.bfloat16, jnp.float32
     S = jax.ShapeDtypeStruct
-    near = (lax.axis_index("xh") * 2 + lax.axis_index("c")).astype(jnp.int32).reshape(1)
+    at = (lax.axis_index("xh") * 2 + lax.axis_index("c")).astype(jnp.int32).reshape(1)
 
     outgoing = call(
-        outgoing_kernel, S((GROUP, D + OWN, TOK), bf16), near, pre_acts, cotangent,
+        outgoing_kernel, S((GROUP, D + OWN, TOK), bf16), at, pre_acts, cotangent,
         scratch=[pltpu.VMEM((FFH, TOK), bf16)],
     )
     incoming = lax.all_to_all(outgoing, GROUP_AXES, 0, 0)
     block = (FAR, ROWS, LANES)
-    dh, own, *parts = call(
+    dh, keep, give = call(
         lambda *refs: products_kernel(scale, *refs),
-        (S((GROUP, OWN, TOK), f32), S(block, f32)) + (S(block, bf16),) * (NEAR - 1),
-        near, incoming, w_out,
+        (S((GROUP, OWN, TOK), f32), S((2,) + block, f32), S((2,) + block, f32)),
+        at, incoming, w_out,
         flops=4 * OWN * D * TOK * GROUP,
         scratch=[pltpu.VMEM((OWN * COLS + ROWS, LANES), f32), pltpu.VMEM((NEAR,) + block, f32)],
     )
     dh = lax.all_to_all(dh, GROUP_AXES, 0, 0)
-    parts = [lax.ppermute(part, NEAR_AXES, [(i, i ^ (j + 1)) for i in range(NEAR)]) for j, part in enumerate(parts)]
+    got = lax.ppermute(give, "c", [(0, 1), (1, 0)])
+    keep, give = call(core_sum_kernel, (S(block, f32), S(block, bf16)), at, keep, got)
+    got = lax.ppermute(give, "xh", [(0, 1), (1, 0)])
     act, slope = call(factors_kernel, (S((TOK, FFH), f32),) * 2, pre_acts)
     d_pre, done = call(d_pre_kernel, (S((TOK, 2 * FFH), bf16), S((ROWS, LANES), f32)), dh.reshape(FFH, TOK), act, slope)
-    summed = call(near_sum_kernel, S(block, bf16), done, own, *parts)
+    summed = call(near_sum_kernel, S(block, bf16), done, keep, got)
     got = lax.all_to_all(summed, "z", 0, 0, axis_index_groups=[FAR_ORDER])
     d_w = call(
-        far_sum_kernel, S((1, PIECE), f32), near, got, scratch=[pltpu.VMEM((1, ROWS * LANES), f32)]
+        far_sum_kernel, S((1, PIECE), f32), at, got, scratch=[pltpu.VMEM((1, ROWS * LANES), f32)]
     )
     return (d_pre, d_w)
 

time: 93.7 us -> 89.6 us (0.956)
  the two profiles are of different devices: /device:TPU:1 before, /device:TPU:6 now
where the time goes in v3:
time: 89.6 us; the launch traced here: 89.2 us
  blocking collectives  66.3 us (74%)
  starting transfers between devices  13.7 us (15%)
  Pallas kernels  4.1 us (5%)
  waiting for transfers between devices  2.45 us (3%)
  local copies, waits for them, and re-layouts  2.01 us (2%)
    all_to_all x1, blocking collectives, body(): got = lax.all_to_all(summed, 'z', 0, 0, axis_index_groups=[FAR_ORDER])  39.4 us
    all_to_all x1, blocking collectives, body(): incoming = lax.all_to_all(outgoing, GROUP_AXES, 0, 0)  26.8 us
    ppermute x1, starting transfers between devices, body(): got = lax.ppermute(give, 'xh', [(0, 1), (1, 0)])  7.05 us
    all_to_all x1, starting transfers between devices, body(): dh = lax.all_to_all(dh, GROUP_AXES, 0, 0)  4.7 us
    pallas_call x7, Pallas kernels, call(): pl.pallas_call(kernel, out_shape=out, in_specs=[SMEM if a.dtype == jnp.in...  4.1 us
    unnamed x8, local copies, waits for them, and re-layouts  2.01 us
    ppermute x1, starting transfers between devices, body(): got = lax.ppermute(give, 'c', [(0, 1), (1, 0)])  1.91 us
  transfers between devices with their start and end apart: 3, of which 2 were waited for; matrix products, arithmetic and copies ran while one was open for 0% of the time, Pallas kernels for 2%

profile of v3, /device:TPU:6, one launch (start us, length us, event | category | flops | bytes accessed | tf_op | source)
XLA Modules:
  0.0 89.2 jit_solution(13304952222065707528)
XLA Ops:
  0.6 0.0 copy-start
  0.6 1.1 %copy-done = bf16[128,2560]{1,0:T(8,128)(2,1)S(1)} copy-done((bf16[128,2560]{1,0:T(8,128)(2,1)S(1)}, bf16[128,2560]{1,0:T(8,128)(2,1)}, u32[]{:S(2)}) %copy-start) | copy-done | bytes 655384
  1.7 0.0 copy-start.3
  1.7 0.9 %copy-done.3 = bf16[128,640]{1,0:T(8,128)(2,1)S(1)} copy-done((bf16[128,640]{1,0:T(8,128)(2,1)S(1)}, bf16[128,640]{1,0:T(8,128)(2,1)}, u32[]{:S(2)}) %copy-start.3) | copy-done | bytes 163864
  2.6 0.4 shard_map.50
  3.1 0.0 copy-start.2
  3.1 26.8 %all_to_all.15.refs_1_ = bf16[8,800,128]{2,1,0:T(8,128)(2,1)S(1)} all-to-all(bf16[8,800,128]{2,1,0:T(8,128)(2,1)S(1)} %shard_map.50), channel_id=1, replica_groups=mesh['z'=32,'xh'=2,'c'=2,'y'=4,'xl'=2] {'y','xl'}, dimensions={0} | all-to-all | bytes 3276800 | tf_op jit(solution)/shard_map/all_to_all | solution.py:143
  29.9 0.0 copy-done.2
  29.9 0.0 copy-start.1
  29.9 1.5 %shard_map.51 = (f32[8,160,128]{2,1,0:T(8,128)}, f32[2,32,8,128]{3,2,1,0:T(8,128)S(1)}, f32[2,32,8,128]{3,2,1,0:T(8,128)S(1)}) custom-call(s32[1]{0:T(128)} %bitcast._.refs_0_.at_ref, bf16[8,800,128]{2,1,0:T(8,128)(2,1)S(1)} %all_to_all.15.refs_1_, bf16[160,640]{1,0:T(8,128)(2,1)S(1)} %copy-done.2), custom_call_target="tpu_custom_call" | custom-call | flops 419430400 | bytes 3022852 | tf_op jit(solution)/shard_map/pallas_call | solution.py:122
  31.5 4.7 %all-to-all-start.1 = ((f32[8,160,128]{2,1,0:T(8,128)}), f32[8,160,128]{2,1,0:T(8,128)S(1)}, u32[]{:S(2)}, u32[]{:S(2)}) async-start(f32[8,160,128]{2,1,0:T(8,128)} %get-tuple-element.11), calls=%async_computation.1 | async-start | bytes 1310720 | tf_op jit(solution)/shard_map/all_to_all | solution.py:152
  36.2 1.9 %collective-permute-start = (f32[2,32,8,128]{3,2,1,0:T(8,128)S(1)}, f32[2,32,8,128]{3,2,1,0:T(8,128)S(1)}, u32[]{:S(2)}, u32[]{:S(2)}) collective-permute-start(f32[2,32,8,128]{3,2,1,0:T(8,128)S(1)} %get-tuple-element.17), channel_id=1, source_target_pairs={{0,8},{8,0},{1,9},{9,1},{2,10},{10,2},{3,11},{11,3},{4,12},{12,4},... | collective-permute-start | bytes 786440 | tf_op jit(solution)/shard_map/ppermute | solution.py:153
  38.1 1.5 %collective-permute-done.got_ref = f32[2,32,8,128]{3,2,1,0:T(8,128)S(1)} collective-permute-done((f32[2,32,8,128]{3,2,1,0:T(8,128)S(1)}, f32[2,32,8,128]{3,2,1,0:T(8,128)S(1)}, u32[]{:S(2)}, u32[]{:S(2)}) %collective-permute-start) | collective-permute-done | bytes 262176 | tf_op jit(solution)/shard_map/ppermute | solution.py:153
  39.6 7.0 %collective-permute-start.1 = (bf16[32,8,128]{2,1,0:T(8,128)(2,1)S(1)}, bf16[32,8,128]{2,1,0:T(8,128)(2,1)S(1)}, u32[]{:S(2)}, u32[]{:S(2)}) collective-permute-start(bf16[32,8,128]{2,1,0:T(8,128)(2,1)S(1)} %get-tuple-element.19), channel_id=1, source_target_pairs={{0,16},{16,0},{1,17},{17,1},{2,18},{18,2},{3,19},{19,3},{4,20},{20... | collective-permute-start | bytes 196616 | tf_op jit(solution)/shard_map/ppermute | solution.py:155
  46.7 0.0 copy-done.1
  46.7 0.3 shard_map.52
  47.0 0.0 all-to-all-done.1
  47.0 1.1 %shard_map.53 = (bf16[128,2560]{1,0:T(8,128)(2,1)}, f32[8,128]{1,0:T(8,128)S(1)}) custom-call(f32[1280,128]{1,0:T(8,128)S(1)} %bitcast.2, f32[128,1280]{1,0:T(8,128)S(1)} %get-tuple-element.12.act_ref, f32[128,1280]{1,0:T(8,128)S(1)} %get-tuple-element.13.slope_ref), custom_call_target="tpu_custom_call" | custom-call | bytes 2625536 | tf_op jit(solution)/shard_map/pallas_call | solution.py:122
  48.1 0.9 %collective-permute-done.1.got_ref = bf16[32,8,128]{2,1,0:T(8,128)(2,1)S(1)} collective-permute-done((bf16[32,8,128]{2,1,0:T(8,128)(2,1)S(1)}, bf16[32,8,128]{2,1,0:T(8,128)(2,1)S(1)}, u32[]{:S(2)}, u32[]{:S(2)}) %collective-permute-start.1) | collective-permute-done | bytes 65568 | tf_op jit(solution)/shard_map/ppermute | solution.py:155
  49.1 39.4 %all_to_all.16.got_ref = bf16[32,8,128]{2,1,0:T(8,128)(2,1)S(1)} all-to-all(bf16[32,8,128]{2,1,0:T(8,128)(2,1)S(1)} %shard_map.55), channel_id=1, replica_groups={{512,544,576,608,640,672,704,736,768,800,832,864,896,928,960,992,0,32,6..., dimensions={0} | all-to-all | bytes 131072 | tf_op jit(solution)/shard_map/all_to_all | solution.py:159
  88.5 0.7 shard_map.56
  (2 shorter events, 0.1 us)
Async XLA Ops:
  0.6 1.1 %copy-start = (bf16[128,2560]{1,0:T(8,128)(2,1)S(1)}, bf16[128,2560]{1,0:T(8,128)(2,1)}, u32[]{:S(2)}) copy-start(bf16[128,2560]{1,0:T(8,128)(2,1)} %pre_ref.3) | copy-start | bytes 1966084
  1.7 0.9 %copy-start.3 = (bf16[128,640]{1,0:T(8,128)(2,1)S(1)}, bf16[128,640]{1,0:T(8,128)(2,1)}, u32[]{:S(2)}) copy-start(bf16[128,640]{1,0:T(8,128)(2,1)} %cot_ref.1) | copy-start | bytes 491524
  3.1 26.9 %copy-start.2 = (bf16[160,640]{1,0:T(8,128)(2,1)S(1)}, bf16[160,640]{1,0:T(8,128)(2,1)}, u32[]{:S(2)}) copy-start(bf16[160,640]{1,0:T(8,128)(2,1)} %refs_2_.1) | copy-start | bytes 614404
  29.9 16.7 %copy-start.1 = (bf16[128,2560]{1,0:T(8,128)(2,1)S(1)}, bf16[128,2560]{1,0:T(8,128)(2,1)}, u32[]{:S(2)}) copy-start(bf16[128,2560]{1,0:T(8,128)(2,1)} %pre_ref.3) | copy-start | bytes 1966084
  31.5 15.6 %all-to-all-start.1 = ((f32[8,160,128]{2,1,0:T(8,128)}), f32[8,160,128]{2,1,0:T(8,128)S(1)}, u32[]{:S(2)}, u32[]{:S(2)}) async-start(f32[8,160,128]{2,1,0:T(8,128)} %get-tuple-element.11), calls=%async_computation.1 | async-start | bytes 1310720 | tf_op jit(solution)/shard_map/all_to_all | solution.py:152
  36.2 3.4 %collective-permute-start = (f32[2,32,8,128]{3,2,1,0:T(8,128)S(1)}, f32[2,32,8,128]{3,2,1,0:T(8,128)S(1)}, u32[]{:S(2)}, u32[]{:S(2)}) collective-permute-start(f32[2,32,8,128]{3,2,1,0:T(8,128)S(1)} %get-tuple-element.17), channel_id=1, source_target_pairs={{0,8},{8,0},{1,9},{9,1},{2,10},{10,2},{3,11},{11,3},{4,12},{12,4},... | collective-permute-start | bytes 786440 | tf_op jit(solution)/shard_map/ppermute | solution.py:153
  39.6 9.4 %collective-permute-start.1 = (bf16[32,8,128]{2,1,0:T(8,128)(2,1)S(1)}, bf16[32,8,128]{2,1,0:T(8,128)(2,1)S(1)}, u32[]{:S(2)}, u32[]{:S(2)}) collective-permute-start(bf16[32,8,128]{2,1,0:T(8,128)(2,1)S(1)} %get-tuple-element.19), channel_id=1, source_target_pairs={{0,16},{16,0},{1,17},{17,1},{2,18},{18,2},{3,19},{19,3},{4,20},{20... | collective-permute-start | bytes 196616 | tf_op jit(solution)/shard_map/ppermute | solution.py:155

commit v4 on v3

--- a/solution.py
+++ b/solution.py
@@ -22,9 +22,11 @@
 GROUP_AXES = ("y", "xl")
 NEAR_AXES = ("xh", "c")
 FAR_AXES = ("z",)
+GROUP_ORDER = [5, 4, 7, 6, 1, 0, 3, 2]
 FAR_ORDER = [(i + 16) % FAR for i in range(FAR)]
 DP_AXES = FAR_AXES + NEAR_AXES
 VMEM = pl.BlockSpec(memory_space=pltpu.VMEM)
+ANY = pl.BlockSpec(memory_space=pl.ANY)
 SMEM = pl.BlockSpec(memory_space=pltpu.SMEM)
 
 
@@ -32,11 +34,19 @@
     return 0.5 * (1.0 + lax.erf(gate * (1.0 / math.sqrt(2.0))))
 
 
-def outgoing_kernel(_, pre_ref, cot_ref, out_ref, ht_ref):
+def outgoing_kernel(_, pre_hbm, cot_hbm, out_hbm, pre_ref, cot_ref, cols_ref, ht_ref, in_sems, out_sems):
+    cot_copy = pltpu.make_async_copy(cot_hbm, cot_ref, in_sems.at[0])
+    cot_copy.start()
+    pre_copy = pltpu.make_async_copy(pre_hbm, pre_ref, in_sems.at[1])
+    pre_copy.start()
+    cot_copy.wait()
     for c in range(COLS):
-        block = cot_ref[:, pl.ds(c * LANES, LANES)]
-        for s in range(GROUP):
-            out_ref[s, pl.ds(c * TOK, TOK), :] = block
+        cols_ref[pl.ds(c * TOK, TOK), :] = cot_ref[:, pl.ds(c * LANES, LANES)]
+    sent = []
+    for s in range(GROUP):
+        sent.append(pltpu.make_async_copy(cols_ref, out_hbm.at[s, pl.ds(0, D), :], out_sems.at[0, s]))
+        sent[-1].start()
+    pre_copy.wait()
     for j in range(FFH // LANES):
         cols = pl.ds(j * LANES, LANES)
         value = pre_ref[:, cols].astype(jnp.float32)
@@ -44,7 +54,11 @@
         hidden = value * (gate * cdf_of(gate))
         ht_ref[cols, :] = hidden.T.astype(jnp.bfloat16)
     for s in range(GROUP):
-        out_ref[s, pl.ds(D, OWN), :] = ht_ref[pl.ds(s * OWN, OWN), :]
+        rows = ht_ref.at[pl.ds(GROUP_ORDER[s] * OWN, OWN), :]
+        sent.append(pltpu.make_async_copy(rows, out_hbm.at[s, pl.ds(D, OWN), :], out_sems.at[1, s]))
+        sent[-1].start()
+    for copy in sent:
+        copy.wait()
 
 
 def factors_kernel(pre_ref, act_ref, slope_ref):
@@ -58,7 +72,7 @@
         slope_ref[:, cols] = value * (cdf + gate * dens)
 
 
-def products_kernel(scale, at_ref, in_ref, w_ref, dh_ref, keep_ref, give_ref, flat_ref, parts_ref):
+def products_kernel(scale, at_ref, in_ref, w_ref, dh_hbm, keep_ref, give_ref, flat_ref, parts_ref, dh_ref, sem):
     cots = jnp.concatenate(
         [
             jnp.concatenate([in_ref[s, pl.ds(c * TOK, TOK), :] for c in range(COLS)], axis=1)
@@ -68,7 +82,9 @@
     )
     dht = lax.dot_general(w_ref[...], cots, (((1,), (1,)), ((), ())), preferred_element_type=jnp.float32)
     for s in range(GROUP):
-        dh_ref[s] = dht[:, s * TOK : (s + 1) * TOK]
+        dh_ref[GROUP_ORDER[s]] = dht[:, s * TOK : (s + 1) * TOK]
+    dh_copy = pltpu.make_async_copy(dh_ref, dh_hbm, sem)
+    dh_copy.start()
     ht = jnp.concatenate([in_ref[s, pl.ds(D, OWN), :] for s in range(GROUP)], axis=1)
     total = jnp.dot(ht, cots, preferred_element_type=jnp.float32) * scale
     for c in range(COLS):
@@ -82,6 +98,7 @@
     for half in range(2):
         keep_ref[half] = parts_ref[half * 2 + core]
         give_ref[half] = parts_ref[half * 2 + 1 - core]
+    dh_copy.wait()
 
 
 def core_sum_kernel(at_ref, own_ref, got_ref, keep_ref, give_ref):
@@ -116,15 +133,16 @@
             out_ref[...] = line_ref[:, pl.ds(near * PIECE % LANES, PIECE)]
 
 
-def call(kernel, out, *args, flops=0, scratch=()):
+def call(kernel, out, *args, flops=0, scratch=(), raw=(), raw_out=False, vmem=16 << 20):
     outs = out if isinstance(out, tuple) else (out,)
     moved = sum(a.size * a.dtype.itemsize for a in args) + sum(o.size * o.dtype.itemsize for o in outs)
+    first = ANY if raw_out else VMEM
     return pl.pallas_call(
         kernel,
         out_shape=out,
-        in_specs=[SMEM if a.dtype == jnp.int32 else VMEM for a in args],
-        out_specs=(VMEM,) * len(outs) if isinstance(out, tuple) else VMEM,
-        compiler_params=pltpu.CompilerParams(vmem_limit_bytes=16 << 20),
+        in_specs=[ANY if i in raw else SMEM if a.dtype == jnp.int32 else VMEM for i, a in enumerate(args)],
+        out_specs=(first,) + (VMEM,) * (len(outs) - 1) if isinstance(out, tuple) else first,
+        compiler_params=pltpu.CompilerParams(vmem_limit_bytes=vmem),
         cost_estimate=pl.CostEstimate(flops=flops, bytes_accessed=moved, transcendentals=0),
         scratch_shapes=list(scratch),
     )(*args)
@@ -138,16 +156,32 @@
 
     outgoing = call(
         outgoing_kernel, S((GROUP, D + OWN, TOK), bf16), at, pre_acts, cotangent,
-        scratch=[pltpu.VMEM((FFH, TOK), bf16)],
-    )
-    incoming = lax.all_to_all(outgoing, GROUP_AXES, 0, 0)
+        scratch=[
+            pltpu.VMEM((TOK, 2 * FFH), bf16),
+            pltpu.VMEM((TOK, D), bf16),
+            pltpu.VMEM((D, LANES), bf16),
+            pltpu.VMEM((FFH, TOK), bf16),
+            pltpu.SemaphoreType.DMA((2,)),
+            pltpu.SemaphoreType.DMA((2, GROUP)),
+        ],
+        raw=(1, 2),
+        raw_out=True,
+        vmem=60 << 20,
+    )
+    incoming = lax.all_to_all(outgoing, GROUP_AXES, 0, 0, axis_index_groups=[GROUP_ORDER])
     block = (FAR, ROWS, LANES)
     dh, keep, give = call(
         lambda *refs: products_kernel(scale, *refs),
         (S((GROUP, OWN, TOK), f32), S((2,) + block, f32), S((2,) + block, f32)),
         at, incoming, w_out,
         flops=4 * OWN * D * TOK * GROUP,
-        scratch=[pltpu.VMEM((OWN * COLS + ROWS, LANES), f32), pltpu.VMEM((NEAR,) + block, f32)],
+        scratch=[
+            pltpu.VMEM((OWN * COLS + ROWS, LANES), f32),
+            pltpu.VMEM((NEAR,) + block, f32),
+            pltpu.VMEM((GROUP, OWN, TOK), f32),
+            pltpu.SemaphoreType.DMA,
+        ],
+        raw_out=True,
     )
     dh = lax.all_to_all(dh, GROUP_AXES, 0, 0)
     got = lax.ppermute(give, "c", [(0, 1), (1, 0)])

time: 89.6 us -> 89.9 us (level)
  starting transfers between devices: 13.7 us -> 17.3 us
  blocking collectives: 66.3 us -> 63 us
  local copies, waits for them, and re-layouts: 2.01 us -> 0.01 us
  Pallas kernels: 4.1 us -> 6.01 us
    ppermute x1, starting transfers between devices: 7.05 us -> 9.9 us  [body(): got = lax.ppermute(give, 'xh', [(0, 1), (1, 0)])]
    all_to_all x1, blocking collectives: 39.4 us -> 36.6 us  [body(): got = lax.all_to_all(summed, 'z', 0, 0, axis_index_groups=[FAR_ORDER])]
    unnamed x8 -> x4, local copies, waits for them, and re-layouts: 2.01 us -> 0.01 us
    pallas_call x7, Pallas kernels: 4.1 us -> 6.01 us  [call(): pl.pallas_call(kernel, out_shape=out, in_specs=[ANY if i in raw else SMEM...]
where the time goes in v4:
time: 89.9 us; the launch traced here: 89.5 us
  blocking collectives  63 us (70%)
  starting transfers between devices  17.3 us (19%)
  Pallas kernels  6.01 us (7%)
  waiting for transfers between devices  2.45 us (3%)
    all_to_all x1, blocking collectives, body(): got = lax.all_to_all(summed, 'z', 0, 0, axis_index_groups=[FAR_ORDER])  36.6 us
    all_to_all x1, blocking collectives, body(): lax.all_to_all(outgoing, GROUP_AXES, 0, 0, axis_index_groups=[GROUP_ORDER])  26.4 us
    ppermute x1, starting transfers between devices, body(): got = lax.ppermute(give, 'xh', [(0, 1), (1, 0)])  9.9 us
    pallas_call x7, Pallas kernels, call(): pl.pallas_call(kernel, out_shape=out, in_specs=[ANY if i in raw else SMEM...  6.01 us
    all_to_all x1, starting transfers between devices, body(): dh = lax.all_to_all(dh, GROUP_AXES, 0, 0)  5.54 us
    ppermute x1, starting transfers between devices, body(): got = lax.ppermute(give, 'c', [(0, 1), (1, 0)])  1.91 us
  transfers between devices with their start and end apart: 3, of which 2 were waited for; matrix products, arithmetic and copies ran while one was open for 0% of the time, Pallas kernels for 2%

profile of v4, /device:TPU:6, one launch (start us, length us, event | category | flops | bytes accessed | tf_op | source)
XLA Modules:
  0.0 89.5 jit_solution(14621184412645457135)
XLA Ops:
  0.6 2.4 %shard_map.50 = bf16[8,800,128]{2,1,0:T(8,128)(2,1)} custom-call(s32[1]{0:T(128)} %bitcast._.refs_0_.at_ref, bf16[128,2560]{1,0:T(8,128)(2,1)} %pre_ref.1, bf16[128,640]{1,0:T(8,128)(2,1)} %cot_hbm.1), custom_call_target="tpu_custom_call" | custom-call | bytes 2457604 | tf_op jit(solution)/shard_map/pallas_call | solution.py:140
  3.0 0.0 copy-start.1
  3.0 26.4 %all_to_all.15.refs_1_ = bf16[8,800,128]{2,1,0:T(8,128)(2,1)S(1)} all-to-all(bf16[8,800,128]{2,1,0:T(8,128)(2,1)} %shard_map.50), channel_id=1, replica_groups={{5,4,7,6,1,0,3,2},{13,12,15,14,9,8,11,10},{21,20,23,22,17,16,19,18},{29..., dimensions={0} | all-to-all | bytes 3276800 | tf_op jit(solution)/shard_map/all_to_all | solution.py:171
  29.5 0.0 copy-done.1
  29.5 0.0 copy-start
  29.5 1.5 %shard_map.51 = (f32[8,160,128]{2,1,0:T(8,128)}, f32[2,32,8,128]{3,2,1,0:T(8,128)S(1)}, f32[2,32,8,128]{3,2,1,0:T(8,128)S(1)}) custom-call(s32[1]{0:T(128)} %bitcast._.refs_0_.at_ref, bf16[8,800,128]{2,1,0:T(8,128)(2,1)S(1)} %all_to_all.15.refs_1_, bf16[160,640]{1,0:T(8,128)(2,1)S(1)} %copy-done.1), custom_call_target="tpu_custom_call" | custom-call | flops 419430400 | bytes 3022852 | tf_op jit(solution)/shard_map/pallas_call | solution.py:140
  31.0 5.5 %all-to-all-start.1 = ((f32[8,160,128]{2,1,0:T(8,128)}), f32[8,160,128]{2,1,0:T(8,128)S(1)}, u32[]{:S(2)}, u32[]{:S(2)}) async-start(f32[8,160,128]{2,1,0:T(8,128)} %get-tuple-element.11), calls=%async_computation.1 | async-start | bytes 1310720 | tf_op jit(solution)/shard_map/all_to_all | solution.py:186
  36.5 1.9 %collective-permute-start = (f32[2,32,8,128]{3,2,1,0:T(8,128)S(1)}, f32[2,32,8,128]{3,2,1,0:T(8,128)S(1)}, u32[]{:S(2)}, u32[]{:S(2)}) collective-permute-start(f32[2,32,8,128]{3,2,1,0:T(8,128)S(1)} %get-tuple-element.17), channel_id=1, source_target_pairs={{0,8},{8,0},{1,9},{9,1},{2,10},{10,2},{3,11},{11,3},{4,12},{12,4},... | collective-permute-start | bytes 786440 | tf_op jit(solution)/shard_map/ppermute | solution.py:187
  38.4 1.5 %collective-permute-done.got_ref = f32[2,32,8,128]{3,2,1,0:T(8,128)S(1)} collective-permute-done((f32[2,32,8,128]{3,2,1,0:T(8,128)S(1)}, f32[2,32,8,128]{3,2,1,0:T(8,128)S(1)}, u32[]{:S(2)}, u32[]{:S(2)}) %collective-permute-start) | collective-permute-done | bytes 262176 | tf_op jit(solution)/shard_map/ppermute | solution.py:187
  40.0 9.9 %collective-permute-start.1 = (bf16[32,8,128]{2,1,0:T(8,128)(2,1)S(1)}, bf16[32,8,128]{2,1,0:T(8,128)(2,1)S(1)}, u32[]{:S(2)}, u32[]{:S(2)}) collective-permute-start(bf16[32,8,128]{2,1,0:T(8,128)(2,1)S(1)} %get-tuple-element.19), channel_id=1, source_target_pairs={{0,16},{16,0},{1,17},{17,1},{2,18},{18,2},{3,19},{19,3},{4,20},{20... | collective-permute-start | bytes 196616 | tf_op jit(solution)/shard_map/ppermute | solution.py:189
  49.9 0.0 copy-done
  49.9 0.3 shard_map.52
  50.2 0.0 all-to-all-done.1
  50.2 1.1 %shard_map.53 = (bf16[128,2560]{1,0:T(8,128)(2,1)}, f32[8,128]{1,0:T(8,128)S(1)}) custom-call(f32[1280,128]{1,0:T(8,128)S(1)} %bitcast.2, f32[128,1280]{1,0:T(8,128)S(1)} %get-tuple-element.12.act_ref, f32[128,1280]{1,0:T(8,128)S(1)} %get-tuple-element.13.slope_ref), custom_call_target="tpu_custom_call" | custom-call | bytes 2625536 | tf_op jit(solution)/shard_map/pallas_call | solution.py:140
  51.3 0.9 %collective-permute-done.1.got_ref = bf16[32,8,128]{2,1,0:T(8,128)(2,1)S(1)} collective-permute-done((bf16[32,8,128]{2,1,0:T(8,128)(2,1)S(1)}, bf16[32,8,128]{2,1,0:T(8,128)(2,1)S(1)}, u32[]{:S(2)}, u32[]{:S(2)}) %collective-permute-start.1) | collective-permute-done | bytes 65568 | tf_op jit(solution)/shard_map/ppermute | solution.py:189
  52.3 36.6 %all_to_all.16.got_ref = bf16[32,8,128]{2,1,0:T(8,128)(2,1)S(1)} all-to-all(bf16[32,8,128]{2,1,0:T(8,128)(2,1)S(1)} %shard_map.55), channel_id=1, replica_groups={{512,544,576,608,640,672,704,736,768,800,832,864,896,928,960,992,0,32,6..., dimensions={0} | all-to-all | bytes 131072 | tf_op jit(solution)/shard_map/all_to_all | solution.py:193
  88.9 0.7 shard_map.56
  (2 shorter events, 0.0 us)
Async XLA Ops:
  3.0 26.5 %copy-start.1 = (bf16[160,640]{1,0:T(8,128)(2,1)S(1)}, bf16[160,640]{1,0:T(8,128)(2,1)}, u32[]{:S(2)}) copy-start(bf16[160,640]{1,0:T(8,128)(2,1)} %refs_2_.1) | copy-start | bytes 614404
  29.5 20.4 %copy-start = (bf16[128,2560]{1,0:T(8,128)(2,1)S(1)}, bf16[128,2560]{1,0:T(8,128)(2,1)}, u32[]{:S(2)}) copy-start(bf16[128,2560]{1,0:T(8,128)(2,1)} %pre_ref.1) | copy-start | bytes 1966084
  31.0 19.2 %all-to-all-start.1 = ((f32[8,160,128]{2,1,0:T(8,128)}), f32[8,160,128]{2,1,0:T(8,128)S(1)}, u32[]{:S(2)}, u32[]{:S(2)}) async-start(f32[8,160,128]{2,1,0:T(8,128)} %get-tuple-element.11), calls=%async_computation.1 | async-start | bytes 1310720 | tf_op jit(solution)/shard_map/all_to_all | solution.py:186
  36.5 3.4 %collective-permute-start = (f32[2,32,8,128]{3,2,1,0:T(8,128)S(1)}, f32[2,32,8,128]{3,2,1,0:T(8,128)S(1)}, u32[]{:S(2)}, u32[]{:S(2)}) collective-permute-start(f32[2,32,8,128]{3,2,1,0:T(8,128)S(1)} %get-tuple-element.17), channel_id=1, source_target_pairs={{0,8},{8,0},{1,9},{9,1},{2,10},{10,2},{3,11},{11,3},{4,12},{12,4},... | collective-permute-start | bytes 786440 | tf_op jit(solution)/shard_map/ppermute | solution.py:187
  40.0 12.3 %collective-permute-start.1 = (bf16[32,8,128]{2,1,0:T(8,128)(2,1)S(1)}, bf16[32,8,128]{2,1,0:T(8,128)(2,1)S(1)}, u32[]{:S(2)}, u32[]{:S(2)}) collective-permute-start(bf16[32,8,128]{2,1,0:T(8,128)(2,1)S(1)} %get-tuple-element.19), channel_id=1, source_target_pairs={{0,16},{16,0},{1,17},{17,1},{2,18},{18,2},{3,19},{19,3},{4,20},{20... | collective-permute-start | bytes 196616 | tf_op jit(solution)/shard_map/ppermute | solution.py:189

commit v5 on v3

--- a/solution.py
+++ b/solution.py
@@ -47,7 +47,8 @@
         out_ref[s, pl.ds(D, OWN), :] = ht_ref[pl.ds(s * OWN, OWN), :]
 
 
-def factors_kernel(pre_ref, act_ref, slope_ref):
+def factors_kernel(pre_ref, act_ref, slope_ref, done_ref):
+    done_ref[...] = jnp.zeros_like(done_ref)
     for j in range(FFH // LANES):
         cols = pl.ds(j * LANES, LANES)
         value = pre_ref[:, cols].astype(jnp.float32)
@@ -94,8 +95,12 @@
     out_ref[...] = (own_ref[...] + got_ref[...].astype(jnp.float32)).astype(jnp.bfloat16)
 
 
-def d_pre_kernel(dh_ref, act_ref, slope_ref, out_ref, done_ref):
-    done_ref[...] = jnp.zeros_like(done_ref)
+def last_kernel(at_ref, got_ref, dh_ref, act_ref, slope_ref, d_pre_ref, d_w_ref, line_ref):
+    d_pre_part(dh_ref, act_ref, slope_ref, d_pre_ref)
+    far_sum_part(at_ref, got_ref, d_w_ref, line_ref)
+
+
+def d_pre_part(dh_ref, act_ref, slope_ref, out_ref):
     for j in range(FFH // LANES):
         cols = pl.ds(j * LANES, LANES)
         dh = dh_ref[cols, :].T
@@ -103,7 +108,7 @@
         out_ref[:, pl.ds(FFH + j * LANES, LANES)] = (dh * slope_ref[:, cols]).astype(jnp.bfloat16)
 
 
-def far_sum_kernel(at_ref, got_ref, out_ref, line_ref):
+def far_sum_part(at_ref, got_ref, out_ref, line_ref):
     total = jnp.zeros((ROWS, LANES), jnp.float32)
     for far in range(FAR):
         total += got_ref[far].astype(jnp.float32)
@@ -137,7 +142,7 @@
     at = (lax.axis_index("xh") * 2 + lax.axis_index("c")).astype(jnp.int32).reshape(1)
 
     outgoing = call(
-        outgoing_kernel, S((GROUP, D + OWN, TOK), bf16), at, pre_acts, cotangent,
+        outgoing_kernel, S((GROUP, D + OWN, TOK), bf16), at, pltpu.with_memory_space_constraint(pre_acts, pltpu.HBM), pltpu.with_memory_space_constraint(cotangent, pltpu.HBM),
         scratch=[pltpu.VMEM((FFH, TOK), bf16)],
     )
     incoming = lax.all_to_all(outgoing, GROUP_AXES, 0, 0)
@@ -153,12 +158,12 @@
     got = lax.ppermute(give, "c", [(0, 1), (1, 0)])
     keep, give = call(core_sum_kernel, (S(block, f32), S(block, bf16)), at, keep, got)
     got = lax.ppermute(give, "xh", [(0, 1), (1, 0)])
-    act, slope = call(factors_kernel, (S((TOK, FFH), f32),) * 2, pre_acts)
-    d_pre, done = call(d_pre_kernel, (S((TOK, 2 * FFH), bf16), S((ROWS, LANES), f32)), dh.reshape(FFH, TOK), act, slope)
+    act, slope, done = call(factors_kernel, (S((TOK, FFH), f32), S((TOK, FFH), f32), S((ROWS, LANES), f32)), pre_acts)
     summed = call(near_sum_kernel, S(block, bf16), done, keep, got)
     got = lax.all_to_all(summed, "z", 0, 0, axis_index_groups=[FAR_ORDER])
-    d_w = call(
-        far_sum_kernel, S((1, PIECE), f32), at, got, scratch=[pltpu.VMEM((1, ROWS * LANES), f32)]
+    d_pre, d_w = call(
+        last_kernel, (S((TOK, 2 * FFH), bf16), S((1, PIECE), f32)), at, got, dh.reshape(FFH, TOK), act, slope,
+        scratch=[pltpu.VMEM((1, ROWS * LANES), f32)],
     )
     return (d_pre, d_w)
 

time: 89.6 us -> 89.1 us (level)
  local copies, waits for them, and re-layouts: 2.01 us -> 0.01 us
  waiting for transfers between devices: 2.45 us -> 3.54 us
    unnamed x8 -> x4, local copies, waits for them, and re-layouts: 2.01 us -> 0.01 us
    ppermute x1, waiting for transfers between devices: 0.95 us -> 2.04 us  [body(): got = lax.ppermute(give, 'xh', [(0, 1), (1, 0)])]
    pallas_call x7 -> x6, Pallas kernels: 4.1 us -> 4.61 us  [call(): pl.pallas_call(kernel, out_shape=out, in_specs=[SMEM if a.dtype == jnp.in...]
  transfers between devices with their start and end apart: 3 -> 3, of which waited for: 2 -> 2; matrix products, arithmetic and copies ran while one was open for 0% -> 0% of each run, Pallas kernels for 2% -> 0%
where the time goes in v5:
time: 89.1 us; the launch traced here: 88.8 us
  blocking collectives  66.3 us (74%)
  starting transfers between devices  13.7 us (15%)
  Pallas kernels  4.61 us (5%)
  waiting for transfers between devices  3.54 us (4%)
    all_to_all x1, blocking collectives, body(): got = lax.all_to_all(summed, 'z', 0, 0, axis_index_groups=[FAR_ORDER])  39.4 us
    all_to_all x1, blocking collectives, body(): incoming = lax.all_to_all(outgoing, GROUP_AXES, 0, 0)  26.8 us
    ppermute x1, starting transfers between devices, body(): got = lax.ppermute(give, 'xh', [(0, 1), (1, 0)])  7.05 us
    all_to_all x1, starting transfers between devices, body(): dh = lax.all_to_all(dh, GROUP_AXES, 0, 0)  4.7 us
    pallas_call x6, Pallas kernels, call(): pl.pallas_call(kernel, out_shape=out, in_specs=[SMEM if a.dtype == jnp.in...  4.61 us
    ppermute x1, waiting for transfers between devices, body(): got = lax.ppermute(give, 'xh', [(0, 1), (1, 0)])  2.04 us
    ppermute x1, starting transfers between devices, body(): got = lax.ppermute(give, 'c', [(0, 1), (1, 0)])  1.91 us
  transfers between devices with their start and end apart: 3, of which 2 were waited for; matrix products, arithmetic and copies ran while one was open for 0% of the time, Pallas kernels for 0%

profile of v5, /device:TPU:6, one launch (start us, length us, event | category | flops | bytes accessed | tf_op | source)
XLA Modules:
  0.0 88.8 jit_solution(11612798877666538467)
XLA Ops:
  0.6 1.6 %shard_map.51 = bf16[8,800,128]{2,1,0:T(8,128)(2,1)S(1)} custom-call(s32[1]{0:T(128)} %bitcast._.refs_0_.at_ref, bf16[128,2560]{1,0:T(8,128)(2,1)} %pre_ref.3, bf16[128,640]{1,0:T(8,128)(2,1)} %cot_ref.1), custom_call_target="tpu_custom_call" | custom-call | bytes 2457604 | tf_op jit(solution)/shard_map/pallas_call | solution.py:127
  2.2 0.0 copy-start.1
  2.2 26.8 %all_to_all.15.refs_1_ = bf16[8,800,128]{2,1,0:T(8,128)(2,1)S(1)} all-to-all(bf16[8,800,128]{2,1,0:T(8,128)(2,1)S(1)} %shard_map.51), channel_id=1, replica_groups=mesh['z'=32,'xh'=2,'c'=2,'y'=4,'xl'=2] {'y','xl'}, dimensions={0} | all-to-all | bytes 3276800 | tf_op jit(solution)/shard_map/all_to_all | solution.py:148
  29.1 0.0 copy-done.1
  29.1 0.0 copy-start
  29.1 1.5 %shard_map.52 = (f32[8,160,128]{2,1,0:T(8,128)}, f32[2,32,8,128]{3,2,1,0:T(8,128)S(1)}, f32[2,32,8,128]{3,2,1,0:T(8,128)S(1)}) custom-call(s32[1]{0:T(128)} %bitcast._.refs_0_.at_ref, bf16[8,800,128]{2,1,0:T(8,128)(2,1)S(1)} %all_to_all.15.refs_1_, bf16[160,640]{1,0:T(8,128)(2,1)S(1)} %copy-done.1), custom_call_target="tpu_custom_call" | custom-call | flops 419430400 | bytes 3022852 | tf_op jit(solution)/shard_map/pallas_call | solution.py:127
  30.6 4.7 %all-to-all-start.2 = ((f32[8,160,128]{2,1,0:T(8,128)}), f32[8,160,128]{2,1,0:T(8,128)S(1)}, u32[]{:S(2)}, u32[]{:S(2)}) async-start(f32[8,160,128]{2,1,0:T(8,128)} %get-tuple-element.15), calls=%async_computation.2 | async-start | bytes 1310720 | tf_op jit(solution)/shard_map/all_to_all | solution.py:157
  35.3 1.9 %collective-permute-start = (f32[2,32,8,128]{3,2,1,0:T(8,128)S(1)}, f32[2,32,8,128]{3,2,1,0:T(8,128)S(1)}, u32[]{:S(2)}, u32[]{:S(2)}) collective-permute-start(f32[2,32,8,128]{3,2,1,0:T(8,128)S(1)} %get-tuple-element.12), channel_id=1, source_target_pairs={{0,8},{8,0},{1,9},{9,1},{2,10},{10,2},{3,11},{11,3},{4,12},{12,4},... | collective-permute-start | bytes 786440 | tf_op jit(solution)/shard_map/ppermute | solution.py:158
  37.2 1.5 %collective-permute-done.got_ref = f32[2,32,8,128]{3,2,1,0:T(8,128)S(1)} collective-permute-done((f32[2,32,8,128]{3,2,1,0:T(8,128)S(1)}, f32[2,32,8,128]{3,2,1,0:T(8,128)S(1)}, u32[]{:S(2)}, u32[]{:S(2)}) %collective-permute-start) | collective-permute-done | bytes 262176 | tf_op jit(solution)/shard_map/ppermute | solution.py:158
  38.7 7.1 %collective-permute-start.1 = (bf16[32,8,128]{2,1,0:T(8,128)(2,1)S(1)}, bf16[32,8,128]{2,1,0:T(8,128)(2,1)S(1)}, u32[]{:S(2)}, u32[]{:S(2)}) collective-permute-start(bf16[32,8,128]{2,1,0:T(8,128)(2,1)S(1)} %get-tuple-element.14), channel_id=1, source_target_pairs={{0,16},{16,0},{1,17},{17,1},{2,18},{18,2},{3,19},{19,3},{4,20},{20... | collective-permute-start | bytes 196616 | tf_op jit(solution)/shard_map/ppermute | solution.py:160
  45.8 0.0 copy-done
  45.8 0.3 shard_map.50
  46.1 2.0 %collective-permute-done.1.got_ref = bf16[32,8,128]{2,1,0:T(8,128)(2,1)S(1)} collective-permute-done((bf16[32,8,128]{2,1,0:T(8,128)(2,1)S(1)}, bf16[32,8,128]{2,1,0:T(8,128)(2,1)S(1)}, u32[]{:S(2)}, u32[]{:S(2)}) %collective-permute-start.1) | collective-permute-done | bytes 65568 | tf_op jit(solution)/shard_map/ppermute | solution.py:160
  48.2 0.0 all-to-all-done.2
  48.2 39.4 %all_to_all.16.got_ref = bf16[32,8,128]{2,1,0:T(8,128)(2,1)S(1)} all-to-all(bf16[32,8,128]{2,1,0:T(8,128)(2,1)S(1)} %shard_map.54), channel_id=1, replica_groups={{512,544,576,608,640,672,704,736,768,800,832,864,896,928,960,992,0,32,6..., dimensions={0} | all-to-all | bytes 131072 | tf_op jit(solution)/shard_map/all_to_all | solution.py:163
  87.6 1.2 %shard_map.55 = (bf16[128,2560]{1,0:T(8,128)(2,1)}, f32[1,800]{1,0:T(1,128)}) custom-call(s32[1]{0:T(128)} %bitcast._.refs_0_.at_ref, bf16[32,8,128]{2,1,0:T(8,128)(2,1)S(1)} %all_to_all.16.got_ref, f32[1280,128]{1,0:T(8,128)S(1)} %bitcast.2, f32[128,1280]{1,0:T(8,128)S(1)} %get-tuple-element.16.act_ref, f32[128,1280]{1,0:T(8,128)S(1)} %get-tuple-element.17.slope_ref), custom_call_target="tpu_custom_call" | custom-call | bytes 2690180 | tf_op jit(solution)/shard_map/pallas_call | solution.py:127
  (2 shorter events, 0.1 us)
Async XLA Ops:
  2.2 26.9 %copy-start.1 = (bf16[160,640]{1,0:T(8,128)(2,1)S(1)}, bf16[160,640]{1,0:T(8,128)(2,1)}, u32[]{:S(2)}) copy-start(bf16[160,640]{1,0:T(8,128)(2,1)} %refs_2_.1) | copy-start | bytes 614404
  29.1 16.7 %copy-start = (bf16[128,2560]{1,0:T(8,128)(2,1)S(1)}, bf16[128,2560]{1,0:T(8,128)(2,1)}, u32[]{:S(2)}) copy-start(bf16[128,2560]{1,0:T(8,128)(2,1)} %pre_ref.3) | copy-start | bytes 1966084
  30.6 17.6 %all-to-all-start.2 = ((f32[8,160,128]{2,1,0:T(8,128)}), f32[8,160,128]{2,1,0:T(8,128)S(1)}, u32[]{:S(2)}, u32[]{:S(2)}) async-start(f32[8,160,128]{2,1,0:T(8,128)} %get-tuple-element.15), calls=%async_computation.2 | async-start | bytes 1310720 | tf_op jit(solution)/shard_map/all_to_all | solution.py:157
  35.3 3.4 %collective-permute-start = (f32[2,32,8,128]{3,2,1,0:T(8,128)S(1)}, f32[2,32,8,128]{3,2,1,0:T(8,128)S(1)}, u32[]{:S(2)}, u32[]{:S(2)}) collective-permute-start(f32[2,32,8,128]{3,2,1,0:T(8,128)S(1)} %get-tuple-element.12), channel_id=1, source_target_pairs={{0,8},{8,0},{1,9},{9,1},{2,10},{10,2},{3,11},{11,3},{4,12},{12,4},... | collective-permute-start | bytes 786440 | tf_op jit(solution)/shard_map/ppermute | solution.py:158
  38.7 9.4 %collective-permute-start.1 = (bf16[32,8,128]{2,1,0:T(8,128)(2,1)S(1)}, bf16[32,8,128]{2,1,0:T(8,128)(2,1)S(1)}, u32[]{:S(2)}, u32[]{:S(2)}) collective-permute-start(bf16[32,8,128]{2,1,0:T(8,128)(2,1)S(1)} %get-tuple-element.14), channel_id=1, source_target_pairs={{0,16},{16,0},{1,17},{17,1},{2,18},{18,2},{3,19},{19,3},{4,20},{20... | collective-permute-start | bytes 196616 | tf_op jit(solution)/shard_map/ppermute | solution.py:160

commit v6 on v5

--- a/solution.py
+++ b/solution.py
@@ -22,6 +22,7 @@
 GROUP_AXES = ("y", "xl")
 NEAR_AXES = ("xh", "c")
 FAR_AXES = ("z",)
+GROUP_ORDER = [i ^ 5 for i in range(GROUP)]
 FAR_ORDER = [(i + 16) % FAR for i in range(FAR)]
 DP_AXES = FAR_AXES + NEAR_AXES
 VMEM = pl.BlockSpec(memory_space=pltpu.VMEM)
@@ -44,7 +45,7 @@
         hidden = value * (gate * cdf_of(gate))
         ht_ref[cols, :] = hidden.T.astype(jnp.bfloat16)
     for s in range(GROUP):
-        out_ref[s, pl.ds(D, OWN), :] = ht_ref[pl.ds(s * OWN, OWN), :]
+        out_ref[s, pl.ds(D, OWN), :] = ht_ref[pl.ds(GROUP_ORDER[s] * OWN, OWN), :]
 
 
 def factors_kernel(pre_ref, act_ref, slope_ref, done_ref):
@@ -103,7 +104,9 @@
 def d_pre_part(dh_ref, act_ref, slope_ref, out_ref):
     for j in range(FFH // LANES):
         cols = pl.ds(j * LANES, LANES)
-        dh = dh_ref[cols, :].T
+        units = range(j * LANES, (j + 1) * LANES, 32)
+        rows = [GROUP_ORDER.index(unit // OWN) * OWN + unit % OWN for unit in units]
+        dh = jnp.concatenate([dh_ref[pl.ds(row, 32), :] for row in rows], axis=0).T
         out_ref[:, cols] = (dh * act_ref[:, cols]).astype(jnp.bfloat16)
         out_ref[:, pl.ds(FFH + j * LANES, LANES)] = (dh * slope_ref[:, cols]).astype(jnp.bfloat16)
 
@@ -145,7 +148,7 @@
         outgoing_kernel, S((GROUP, D + OWN, TOK), bf16), at, pltpu.with_memory_space_constraint(pre_acts, pltpu.HBM), pltpu.with_memory_space_constraint(cotangent, pltpu.HBM),
         scratch=[pltpu.VMEM((FFH, TOK), bf16)],
     )
-    incoming = lax.all_to_all(outgoing, GROUP_AXES, 0, 0)
+    incoming = lax.all_to_all(outgoing, GROUP_AXES, 0, 0, axis_index_groups=[GROUP_ORDER])
     block = (FAR, ROWS, LANES)
     dh, keep, give = call(
         lambda *refs: products_kernel(scale, *refs),
@@ -154,7 +157,7 @@
         flops=4 * OWN * D * TOK * GROUP,
         scratch=[pltpu.VMEM((OWN * COLS + ROWS, LANES), f32), pltpu.VMEM((NEAR,) + block, f32)],
     )
-    dh = lax.all_to_all(dh, GROUP_AXES, 0, 0)
+    dh = lax.all_to_all(dh, GROUP_AXES, 0, 0, axis_index_groups=[GROUP_ORDER])
     got = lax.ppermute(give, "c", [(0, 1), (1, 0)])
     keep, give = call(core_sum_kernel, (S(block, f32), S(block, bf16)), at, keep, got)
     got = lax.ppermute(give, "xh", [(0, 1), (1, 0)])

time: 89.1 us -> 89.8 us (level)
  the two profiles are of different devices: /device:TPU:6 before, /device:TPU:4 now
where the time goes in v6:
time: 89.8 us; the launch traced here: 89.5 us
  blocking collectives  62.3 us (69%)
  starting transfers between devices  18.3 us (20%)
  Pallas kernels  4.61 us (5%)
  waiting for transfers between devices  3.54 us (4%)
    all_to_all x1, blocking collectives, body(): got = lax.all_to_all(summed, 'z', 0, 0, axis_index_groups=[FAR_ORDER])  37 us
    all_to_all x1, blocking collectives, body(): lax.all_to_all(outgoing, GROUP_AXES, 0, 0, axis_index_groups=[GROUP_ORDER])  25.3 us
    ppermute x1, starting transfers between devices, body(): got = lax.ppermute(give, 'xh', [(0, 1), (1, 0)])  9.45 us
    all_to_all x1, starting transfers between devices, body(): dh = lax.all_to_all(dh, GROUP_AXES, 0, 0, axis_index_groups=[GROUP_ORDER])  6.94 us
    pallas_call x6, Pallas kernels, call(): pl.pallas_call(kernel, out_shape=out, in_specs=[SMEM if a.dtype == jnp.in...  4.61 us
    ppermute x1, waiting for transfers between devices, body(): got = lax.ppermute(give, 'xh', [(0, 1), (1, 0)])  2.04 us
    ppermute x1, starting transfers between devices, body(): got = lax.ppermute(give, 'c', [(0, 1), (1, 0)])  1.91 us
  transfers between devices with their start and end apart: 3, of which 2 were waited for; matrix products, arithmetic and copies ran while one was open for 0% of the time, Pallas kernels for 0%

profile of v6, /device:TPU:4, one launch (start us, length us, event | category | flops | bytes accessed | tf_op | source)
XLA Modules:
  0.0 89.5 jit_solution(6801460709319673113)
XLA Ops:
  0.6 1.6 %shard_map.51 = bf16[8,800,128]{2,1,0:T(8,128)(2,1)S(1)} custom-call(s32[1]{0:T(128)} %bitcast._.refs_0_.at_ref, bf16[128,2560]{1,0:T(8,128)(2,1)} %pre_ref.3, bf16[128,640]{1,0:T(8,128)(2,1)} %cot_ref.1), custom_call_target="tpu_custom_call" | custom-call | bytes 2457604 | tf_op jit(solution)/shard_map/pallas_call | solution.py:130
  2.2 0.0 copy-start.1
  2.2 25.3 %all_to_all.15.refs_1_ = bf16[8,800,128]{2,1,0:T(8,128)(2,1)S(1)} all-to-all(bf16[8,800,128]{2,1,0:T(8,128)(2,1)S(1)} %shard_map.51), channel_id=1, replica_groups={{5,4,7,6,1,0,3,2},{13,12,15,14,9,8,11,10},{21,20,23,22,17,16,19,18},{29..., dimensions={0} | all-to-all | bytes 3276800 | tf_op jit(solution)/shard_map/all_to_all | solution.py:151
  27.5 0.0 copy-done.1
  27.5 0.0 copy-start
  27.5 1.5 %shard_map.52 = (f32[8,160,128]{2,1,0:T(8,128)}, f32[2,32,8,128]{3,2,1,0:T(8,128)S(1)}, f32[2,32,8,128]{3,2,1,0:T(8,128)S(1)}) custom-call(s32[1]{0:T(128)} %bitcast._.refs_0_.at_ref, bf16[8,800,128]{2,1,0:T(8,128)(2,1)S(1)} %all_to_all.15.refs_1_, bf16[160,640]{1,0:T(8,128)(2,1)S(1)} %copy-done.1), custom_call_target="tpu_custom_call" | custom-call | flops 419430400 | bytes 3022852 | tf_op jit(solution)/shard_map/pallas_call | solution.py:130
  29.0 6.9 %all-to-all-start.2 = ((f32[8,160,128]{2,1,0:T(8,128)}), f32[8,160,128]{2,1,0:T(8,128)S(1)}, u32[]{:S(2)}, u32[]{:S(2)}) async-start(f32[8,160,128]{2,1,0:T(8,128)} %get-tuple-element.15), calls=%async_computation.2 | async-start | bytes 1310720 | tf_op jit(solution)/shard_map/all_to_all | solution.py:160
  36.0 1.9 %collective-permute-start = (f32[2,32,8,128]{3,2,1,0:T(8,128)S(1)}, f32[2,32,8,128]{3,2,1,0:T(8,128)S(1)}, u32[]{:S(2)}, u32[]{:S(2)}) collective-permute-start(f32[2,32,8,128]{3,2,1,0:T(8,128)S(1)} %get-tuple-element.12), channel_id=1, source_target_pairs={{0,8},{8,0},{1,9},{9,1},{2,10},{10,2},{3,11},{11,3},{4,12},{12,4},... | collective-permute-start | bytes 786440 | tf_op jit(solution)/shard_map/ppermute | solution.py:161
  37.9 1.5 %collective-permute-done.got_ref = f32[2,32,8,128]{3,2,1,0:T(8,128)S(1)} collective-permute-done((f32[2,32,8,128]{3,2,1,0:T(8,128)S(1)}, f32[2,32,8,128]{3,2,1,0:T(8,128)S(1)}, u32[]{:S(2)}, u32[]{:S(2)}) %collective-permute-start) | collective-permute-done | bytes 262176 | tf_op jit(solution)/shard_map/ppermute | solution.py:161
  39.4 9.4 %collective-permute-start.1 = (bf16[32,8,128]{2,1,0:T(8,128)(2,1)S(1)}, bf16[32,8,128]{2,1,0:T(8,128)(2,1)S(1)}, u32[]{:S(2)}, u32[]{:S(2)}) collective-permute-start(bf16[32,8,128]{2,1,0:T(8,128)(2,1)S(1)} %get-tuple-element.14), channel_id=1, source_target_pairs={{0,16},{16,0},{1,17},{17,1},{2,18},{18,2},{3,19},{19,3},{4,20},{20... | collective-permute-start | bytes 196616 | tf_op jit(solution)/shard_map/ppermute | solution.py:163
  48.9 0.0 copy-done
  48.9 0.3 shard_map.50
  49.2 2.0 %collective-permute-done.1.got_ref = bf16[32,8,128]{2,1,0:T(8,128)(2,1)S(1)} collective-permute-done((bf16[32,8,128]{2,1,0:T(8,128)(2,1)S(1)}, bf16[32,8,128]{2,1,0:T(8,128)(2,1)S(1)}, u32[]{:S(2)}, u32[]{:S(2)}) %collective-permute-start.1) | collective-permute-done | bytes 65568 | tf_op jit(solution)/shard_map/ppermute | solution.py:163
  51.3 0.0 all-to-all-done.2
  51.3 37.0 %all_to_all.16.got_ref = bf16[32,8,128]{2,1,0:T(8,128)(2,1)S(1)} all-to-all(bf16[32,8,128]{2,1,0:T(8,128)(2,1)S(1)} %shard_map.54), channel_id=1, replica_groups={{512,544,576,608,640,672,704,736,768,800,832,864,896,928,960,992,0,32,6..., dimensions={0} | all-to-all | bytes 131072 | tf_op jit(solution)/shard_map/all_to_all | solution.py:166
  88.3 1.2 %shard_map.55 = (bf16[128,2560]{1,0:T(8,128)(2,1)}, f32[1,800]{1,0:T(1,128)}) custom-call(s32[1]{0:T(128)} %bitcast._.refs_0_.at_ref, bf16[32,8,128]{2,1,0:T(8,128)(2,1)S(1)} %all_to_all.16.got_ref, f32[1280,128]{1,0:T(8,128)S(1)} %bitcast.2, f32[128,1280]{1,0:T(8,128)S(1)} %get-tuple-element.16.act_ref, f32[128,1280]{1,0:T(8,128)S(1)} %get-tuple-element.17.slope_ref), custom_call_target="tpu_custom_call" | custom-call | bytes 2690180 | tf_op jit(solution)/shard_map/pallas_call | solution.py:130
  (2 shorter events, 0.1 us)
Async XLA Ops:
  2.2 25.3 %copy-start.1 = (bf16[160,640]{1,0:T(8,128)(2,1)S(1)}, bf16[160,640]{1,0:T(8,128)(2,1)}, u32[]{:S(2)}) copy-start(bf16[160,640]{1,0:T(8,128)(2,1)} %refs_2_.1) | copy-start | bytes 614404
  27.5 21.4 %copy-start = (bf16[128,2560]{1,0:T(8,128)(2,1)S(1)}, bf16[128,2560]{1,0:T(8,128)(2,1)}, u32[]{:S(2)}) copy-start(bf16[128,2560]{1,0:T(8,128)(2,1)} %pre_ref.3) | copy-start | bytes 1966084
  29.0 22.3 %all-to-all-start.2 = ((f32[8,160,128]{2,1,0:T(8,128)}), f32[8,160,128]{2,1,0:T(8,128)S(1)}, u32[]{:S(2)}, u32[]{:S(2)}) async-start(f32[8,160,128]{2,1,0:T(8,128)} %get-tuple-element.15), calls=%async_computation.2 | async-start | bytes 1310720 | tf_op jit(solution)/shard_map/all_to_all | solution.py:160
  36.0 3.4 %collective-permute-start = (f32[2,32,8,128]{3,2,1,0:T(8,128)S(1)}, f32[2,32,8,128]{3,2,1,0:T(8,128)S(1)}, u32[]{:S(2)}, u32[]{:S(2)}) collective-permute-start(f32[2,32,8,128]{3,2,1,0:T(8,128)S(1)} %get-tuple-element.12), channel_id=1, source_target_pairs={{0,8},{8,0},{1,9},{9,1},{2,10},{10,2},{3,11},{11,3},{4,12},{12,4},... | collective-permute-start | bytes 786440 | tf_op jit(solution)/shard_map/ppermute | solution.py:161
  39.4 11.8 %collective-permute-start.1 = (bf16[32,8,128]{2,1,0:T(8,128)(2,1)S(1)}, bf16[32,8,128]{2,1,0:T(8,128)(2,1)S(1)}, u32[]{:S(2)}, u32[]{:S(2)}) collective-permute-start(bf16[32,8,128]{2,1,0:T(8,128)(2,1)S(1)} %get-tuple-element.14), channel_id=1, source_target_pairs={{0,16},{16,0},{1,17},{17,1},{2,18},{18,2},{3,19},{19,3},{4,20},{20... | collective-permute-start | bytes 196616 | tf_op jit(solution)/shard_map/ppermute | solution.py:163
